TPU v7x, 512 devices: a whole 4x8x8 slice. The times are simulated.
512 devices in a mesh: kv: 64 (over x, z, core), tp: 8 (over y).
Axes of the slice: x: 4, y: 8, z: 8, core: 2. Of those that a mesh axis runs over, the one named last changes fastest.
Arguments:
- queries: bfloat16 [512, 7168], P('kv', 'tp'), may hold values from -30 to 30
- new_keys: bfloat16 [512, 7168], P('kv', 'tp'), may hold values from -6 to 6
- new_values: bfloat16 [512, 7168], P('kv', 'tp'), may hold values from -6 to 6
- keys: bfloat16 [24576, 7168], P('kv', 'tp'), may hold values from -8 to 8
- values: bfloat16 [24576, 7168], P('kv', 'tp'), may hold values from -6 to 6
- slot_request: int32 [24576], P('kv'), may hold values from 0 to 511, as said below
- slot_valid: int32 [24576], P('kv'), may hold values from 0 to 1, as said below
- out_weight: bfloat16 [7168, 7168], P('tp', 'kv'), may hold values from -0.0625 to 0.0625
- out_bias: bfloat16 [7168], P('kv'), may hold values from -3 to 3
- residual: bfloat16 [512, 7168], P('tp', 'kv'), may hold values from -6 to 6
Outputs:
- layer_out: bfloat16 [512, 7168], P('tp', 'kv')
Inputs may be any that keep to these rules, and one draw needn't show every extreme that they name: `slot_request`: slots come in pages of 16 consecutive slots owned by one request; a request's pages are consecutive and may span several holders; every request owns at least one page and at most 514 pages, and one request owns exactly 514. `slot_valid`: only the last page of each request has empty slots, and that page holds at least one cached token in its first slot.
All inputs are finite; a program needn't handle non-finite values.
Results may differ from a plain program's by a relative error of at most 0.0033.
Values may be sent and summed in bfloat16 or wider, within the bound.
A program may use at most 64 MiB of HBM per device.

v0:
```python
import math

import jax
import jax.numpy as jnp
from jax import lax
from jax.sharding import PartitionSpec as P

HD = 128


floor_score = -1e30


def settle(x):
    return lax.optimization_barrier(x.astype(jnp.bfloat16)).astype(jnp.float32)


def normalize(numer, denom, head_count):
    row_total = numer.shape[0]
    quotient = numer.reshape(row_total, head_count, HD) / denom[:, :, None]
    return quotient.reshape(row_total, head_count * HD).astype(jnp.bfloat16)


def on_device(
    queries,
    new_keys,
    new_values,
    keys,
    values,
    slot_request,
    slot_valid,
    out_weight,
    out_bias,
    residual,
):
    head_count = queries.shape[1] // HD
    score_scale = 1.0 / math.sqrt(HD)
    own_rows = queries.shape[0]
    first_row = lax.axis_index("kv") * own_rows
    every_query = lax.all_gather(queries, "kv", axis=0, tiled=True)
    request_count = every_query.shape[0]
    slot_count = keys.shape[0]
    picked = jnp.take(every_query, slot_request, axis=0).reshape(slot_count, head_count, HD)
    scores = (
        jnp.einsum(
            "shd,shd->sh",
            picked,
            keys.reshape(slot_count, head_count, HD),
            preferred_element_type=jnp.float32,
        )
        * score_scale
    )
    live_slot = (slot_valid == 1)[:, None]
    masked = jnp.where(live_slot, scores, floor_score)
    self_scores = (
        jnp.einsum(
            "rhd,rhd->rh",
            queries.reshape(own_rows, head_count, HD),
            new_keys.reshape(own_rows, head_count, HD),
            preferred_element_type=jnp.float32,
        )
        * score_scale
    )
    local_top = (
        jnp.full((request_count, head_count), floor_score, jnp.float32).at[slot_request].max(masked)
    )
    own_top = jnp.maximum(lax.dynamic_slice_in_dim(local_top, first_row, own_rows, 0), self_scores)
    local_top = lax.dynamic_update_slice_in_dim(local_top, own_top, first_row, 0)
    row_top = lax.pmax(local_top, "kv")
    slot_weight = settle(
        jnp.where(live_slot, jnp.exp(masked - jnp.take(row_top, slot_request, axis=0)), 0.0)
    )
    weighted = slot_weight[:, :, None] * values.reshape(slot_count, head_count, HD).astype(
        jnp.float32
    )
    numer_local = jax.ops.segment_sum(
        weighted.reshape(slot_count, head_count * HD), slot_request, num_segments=request_count
    )
    denom_local = jax.ops.segment_sum(slot_weight, slot_request, num_segments=request_count)
    self_weight = settle(
        jnp.exp(self_scores - lax.dynamic_slice_in_dim(row_top, first_row, own_rows, 0))
    )
    self_numer = (
        self_weight[:, :, None] * new_values.reshape(own_rows, head_count, HD).astype(jnp.float32)
    ).reshape(own_rows, head_count * HD)
    numer_local = lax.dynamic_update_slice_in_dim(
        numer_local,
        lax.dynamic_slice_in_dim(numer_local, first_row, own_rows, 0) + self_numer,
        first_row,
        0,
    )
    denom_local = lax.dynamic_update_slice_in_dim(
        denom_local,
        lax.dynamic_slice_in_dim(denom_local, first_row, own_rows, 0) + self_weight,
        first_row,
        0,
    )
    numer, denom = lax.psum((numer_local, denom_local), "kv")
    attended = normalize(numer, denom, head_count)
    projected = lax.psum_scatter(
        jnp.dot(attended, out_weight, preferred_element_type=jnp.float32),
        "tp",
        scatter_dimension=0,
        tiled=True,
    )
    total = residual.astype(jnp.float32) + projected + out_bias.astype(jnp.float32)[None, :]
    return total.astype(jnp.bfloat16)


def solution(mesh):
    placed = (
        P("kv", "tp"),
        P("kv", "tp"),
        P("kv", "tp"),
        P("kv", "tp"),
        P("kv", "tp"),
        P("kv"),
        P("kv"),
        P("tp", "kv"),
        P("kv"),
        P("tp", "kv"),
    )
    return jax.shard_map(
        on_device, mesh=mesh, in_specs=placed, out_specs=P("tp", "kv"), check_vma=False
    )
```

profile of v0, /device:TPU:1, one launch (start us, length us, event | category | flops | bytes accessed | tf_op | source)
XLA Modules:
  0.0 622.5 jit_solution(15484239283756231395)
XLA Ops:
  6.5 0.0 copy-start
  6.5 0.0 all-reduce.2.cloned.1.call-start
  6.5 0.7 compare_select_fusion
  7.3 1.4 copy.13
  8.7 58.0 %all_gather.3 = bf16[512,896]{1,0:T(8,128)(2,1)S(1)} all-gather(bf16[8,896]{1,0:T(8,128)(2,1)} %param.10), channel_id=1, replica_groups=mesh['kv'=64,'tp'=8] {'kv'}, dimensions={0}, use_global_device_ids=true | all-gather | bytes 931840 | tf_op jit(solution)/shard_map/all_gather | solution.py:40
  66.8 0.0 copy-start.7
  66.8 0.0 copy-start.8
  66.8 2.3 gather_fusion
  69.1 0.0 copy-start.3
  69.1 0.0 copy-start.6
  69.1 0.4 copy.12
  69.5 0.0 copy-done.7
  69.5 0.0 copy-done.8
  69.5 0.2 fusion
  69.8 0.0 copy-start.2
  69.8 0.1 copy.24
  69.9 0.0 copy-done.3
  69.9 0.0 copy-done.6
  69.9 0.1 fusion.14
  70.0 0.1 copy.29
  70.1 3.4 scatter_custom_fusion
  73.5 243.3 %pmax.7 = f32[512,7]{1,0:T(8,128)S(1)} all-reduce(f32[512,7]{1,0:T(8,128)S(1)} %maximum_dynamic-update-slice_fusion), channel_id=1, replica_groups=mesh['kv'=64,'tp'=8] {'kv'}, use_global_device_ids=true, to_apply=%region_1.2 | all-reduce | flops 3584 | bytes 28672 | tf_op jit(solution)/shard_map/pmax | solution.py:69
  316.8 1.1 gather_fusion.1
  317.9 0.0 copy-done.2
  317.9 0.4 copy.15
  318.3 0.2 select_convert_fusion
  318.5 0.1 copy.14
  318.6 0.1 bitcast_multiply_fusion
  318.7 0.0 copy-start.5
  318.7 1.5 copy.16
  320.2 0.1 copy.17
  320.3 4.9 scatter_custom_fusion.1
  325.2 0.0 copy-done.5
  325.2 0.1 fusion.13
  325.3 1.3 copy-done.1
  326.5 0.0 all-reduce.2.cloned.1.call-update
  326.6 0.2 reduce-scatter.2.cloned.1.call-start
  326.8 3.3 scatter_custom_fusion.2
  330.1 246.5 %psum.15 = f32[512,7]{1,0:T(8,128)S(1)} all-reduce(f32[512,7]{1,0:T(8,128)S(1)} %add_dynamic-update-slice_fusion), channel_id=1, replica_groups=mesh['kv'=64,'tp'=8] {'kv'}, use_global_device_ids=true, to_apply=%region_5.6 | all-reduce | flops 3584 | bytes 28672 | tf_op jit(solution)/shard_map/psum | solution.py:98
  576.5 0.1 copy.18
  576.6 0.2 div.11
  576.9 1.7 copy.19
  578.6 3.2 fusion.3
  581.8 0.0 reduce-scatter.2.cloned.1.call-update
  581.8 0.0 copy-done.9
  581.8 32.4 %reduce-scatter.2.cloned.1.call-done = f32[64,112]{1,0:T(8,128)} async-done(((f32[512,112]{1,0:T(8,128)}), f32[64,112]{1,0:T(8,128)}) %reduce-scatter.2.cloned.1.call-update) | async-done | bytes 28688 | tf_op jit(solution)/shard_map/reduce_scatter | solution.py:100
  614.3 0.0 copy-done.4
  614.3 1.4 add_convert_fusion
  (11 shorter events, 0.1 us)
Async XLA Ops:
  6.5 572.1 %copy-start = (bf16[896,112]{0,1:T(8,128)(2,1)S(1)}, bf16[896,112]{0,1:T(8,128)(2,1)}, u32[]{:S(2)}) copy-start(bf16[896,112]{0,1:T(8,128)(2,1)} %param.17) | copy-start | bytes 602116
  6.5 572.1 %all-reduce.2.cloned.1.call-start = ((), (), s32[]{:S(2)}) async-start(), calls=%async_computation.1 | async-start | bytes 3670016 | tf_op jit(solution)/shard_map/psum | solution.py:98
  66.8 2.7 copy-start.7
  66.8 2.7 copy-start.8
  69.1 0.8 copy-start.3
  69.1 0.8 copy-start.6
  69.8 248.2 %copy-start.2 = (bf16[384,896]{1,0:T(8,128)(2,1)S(1)}, bf16[384,896]{1,0:T(8,128)(2,1)}, u32[]{:S(2)}) copy-start(bf16[384,896]{1,0:T(8,128)(2,1)} %param.14) | copy-start | bytes 2064388
  318.7 6.5 %copy-start.5 = (bf16[8,896]{1,0:T(8,128)(2,1)S(1)}, bf16[8,896]{1,0:T(8,128)(2,1)}, u32[]{:S(2)}) copy-start(bf16[8,896]{1,0:T(8,128)(2,1)} %param.12) | copy-start | bytes 43012
  325.3 1.3 copy-start.1
  326.6 287.7 %reduce-scatter.2.cloned.1.call-start = ((), (), s32[]{:S(2)}) async-start(), calls=%async_computation.2 | async-start | bytes 294912 | tf_op jit(solution)/shard_map/reduce_scatter | solution.py:100
  578.6 3.2 copy-start.9
  578.6 35.7 %copy-start.4 = (bf16[64,112]{1,0:T(8,128)(2,1)S(1)}, bf16[64,112]{1,0:T(8,128)(2,1)}, u32[]{:S(2)}) copy-start(bf16[64,112]{1,0:T(8,128)(2,1)} %param.19) | copy-start | bytes 43012
Sparse Core Ops, SparseCore 0:
  326.7 197.5 all-reduce.1
  581.9 32.2 reduce-scatter.1
where the time goes:
time: 627 us; the launch traced here: 622 us
  blocking collectives  548 us (87%)
  waiting for transfers between devices  32.5 us (5%)
  other arithmetic  14.4 us (2%)
  between operations  13.6 us (2%)
  local copies, waits for them, and re-layouts  10.8 us (2%)
    psum x1, blocking collectives, on_device(): numer, denom = lax.psum((numer_local, denom_local), 'kv')  246 us
    pmax x1, blocking collectives, on_device(): row_top = lax.pmax(local_top, 'kv')  243 us
    all_gather x1, blocking collectives, on_device(): every_query = lax.all_gather(queries, 'kv', axis=0, tiled=True)  58 us
    reduce_scatter x1, waiting for transfers between devices, on_device(): lax.psum_scatter(jnp.dot(attended, out_weight, preferred_element_type=jnp...  32.4 us
  transfers between devices with their start and end apart: 2, of which 1 were waited for; matrix products, arithmetic and copies ran while one was open for 1% of the time, Pallas kernels for 0%

commit v1 on v0

v1 whole, which is shorter than its diff:
```python
import math

import jax
import jax.numpy as jnp
from jax import lax
from jax.experimental import pallas as pl
from jax.experimental.pallas import tpu as pltpu
from jax.sharding import PartitionSpec as P

HD = 128
HEADS = 7
FEAT = HEADS * HD
WIDE = FEAT + 128
PAGE = 16
NX, NZ, NT, NB = 4, 8, 8, 8
ROWS = 8
FLOOR = -1e30
SCALE = 1.0 / math.sqrt(HD)
MESH = pl.DeviceIdType.MESH
F32, BF16 = jnp.float32, jnp.bfloat16

FAR_FIRST = (4, 3, 5, 2, 6, 1, 7)


def kv_of(x, z, c):
    return (x * NZ + z) * 2 + c


def split3(tile):
    lane = lax.broadcasted_iota(jnp.int32, tile.shape, 1)
    tile = jnp.where(lane < 8, tile, 0.0)
    high = tile.astype(BF16).astype(F32)
    middle = (tile - high).astype(BF16).astype(F32)
    low = tile - high - middle
    return high + pltpu.roll(middle, 8, 1) + pltpu.roll(low, 16, 1)


def join3(tile):
    axis = tile.ndim - 1
    return tile + pltpu.roll(tile, 128 - 8, axis) + pltpu.roll(tile, 128 - 16, axis)


def kernel(
    q_ref, nk_ref, nv_ref, sr_ref, sv_ref, k_hbm, v_hbm, w_hbm, out_ref,
    k_ref, v_ref, w_ref, wg, idc, qz, qs, qr, ob, cb, rb, sb, az, pc, cr, fs, fr,
    local, w_s, w_r, f_s, f_r, id_s, id_r, a1_s, a1_r, a2_s, a2_r, b1_s, b1_r, b2_s, b2_r,
    b3_s, b3_r, c1_s, c1_r, c2_s, c2_r, self_s, self_r,
):
    k = lax.axis_index("kv")
    t = lax.axis_index("tp")
    c = lax.rem(k, 2)
    xz = k // 2
    x = xz // NZ
    z = lax.rem(xz, NZ)
    b = x * 2 + c

    def to_kv(src, dst, send, recv, kv):
        return pltpu.make_async_remote_copy(
            src_ref=src, dst_ref=dst, send_sem=send, recv_sem=recv,
            device_id={"kv": kv}, device_id_type=MESH,
        )

    def to_tp(src, dst, send, recv, tp):
        return pltpu.make_async_remote_copy(
            src_ref=src, dst_ref=dst, send_sem=send, recv_sem=recv,
            device_id={"tp": tp}, device_id_type=MESH,
        )

    def z_at(d):
        return lax.rem(z + d, NZ)

    def b_at(e):
        return lax.rem(b + e, NB)

    def z_peer(d):
        return kv_of(x, z_at(d), c)

    def b_peer(e):
        other = b_at(e)
        return kv_of(other // 2, z, lax.rem(other, 2))

    def x_peer(d):
        return kv_of(lax.rem(x + d, NX), z, c)

    sibling = kv_of(x, z, 1 - c)
    owner = kv_of(lax.rem(z, 4), lax.rem(2 * x + z // 4 + 4, NZ), c)
    band = lax.rem(z + 4, NZ)
    home = kv_of(band // 2, lax.rem(band, 2) * 4 + x, c)

    loads = [
        pltpu.make_async_copy(w_hbm, w_ref, local.at[0]),
        pltpu.make_async_copy(k_hbm, k_ref, local.at[1]),
        pltpu.make_async_copy(v_hbm, v_ref, local.at[2]),
    ]
    for load in loads:
        load.start()

    barrier = pltpu.get_barrier_semaphore()
    for d in range(1, 8):
        pl.semaphore_signal(barrier, inc=1, device_id={"kv": z_peer(d)}, device_id_type=MESH)
        pl.semaphore_signal(barrier, inc=1, device_id={"kv": b_peer(d)}, device_id_type=MESH)
        pl.semaphore_signal(
            barrier, inc=1, device_id={"tp": lax.rem(t + d, NT)}, device_id_type=MESH
        )
    pl.semaphore_signal(barrier, inc=1, device_id={"kv": owner}, device_id_type=MESH)
    pl.semaphore_signal(barrier, inc=1, device_id={"kv": home}, device_id_type=MESH)

    slots = k_ref.shape[0]
    pages = slots // PAGE
    blocks = pages // ROWS
    lane_page = lax.broadcasted_iota(jnp.int32, (pages, slots), 1) // PAGE
    on_page = lane_page == lax.broadcasted_iota(jnp.int32, (pages, slots), 0)
    request_row = jnp.broadcast_to(sr_ref[...].astype(F32), (pages, slots))
    page_request = jnp.max(jnp.where(on_page, request_row, -1.0), axis=1, keepdims=True)
    live = jnp.where(on_page, jnp.broadcast_to(sv_ref[...], (pages, slots)), 0) == 1
    idc[b] = jnp.broadcast_to(page_request, (pages, 128))

    lane8 = lax.broadcasted_iota(jnp.int32, (ROWS, 128), 1)
    own = jnp.zeros((ROWS, 128), F32)
    for h in range(HEADS):
        head = slice(h * HD, (h + 1) * HD)
        product = q_ref[:, head].astype(F32) * nk_ref[:, head].astype(F32)
        own = jnp.where(lane8 == h, jnp.sum(product, axis=1, keepdims=True) * SCALE, own)
    sb[:, :FEAT] = nv_ref[...]
    sb[:, FEAT:] = split3(own).astype(BF16)

    qz[z] = q_ref[...]
    ob[:, blocks:] = jnp.zeros((NB, ob.shape[1] - blocks, ROWS, WIDE), BF16)

    pl.semaphore_wait(barrier, 23)

    sends = []

    def go(copy):
        copy.start()
        sends.append(copy)
        return copy

    a1 = [go(to_kv(q_ref, qz.at[z], a1_s.at[d], a1_r.at[d], z_peer(d))) for d in FAR_FIRST]
    ids = [go(to_kv(idc.at[b], idc.at[b], id_s.at[e], id_r.at[e], b_peer(e))) for e in FAR_FIRST]
    self_copy = go(to_kv(sb, rb.at[NZ], self_s, self_r, owner))
    loads[0].wait()
    columns = w_ref.shape[1]
    wg[b, :, :columns] = w_ref[...]
    wg[b, :, columns:] = jnp.zeros((w_ref.shape[0], 128 - columns), BF16)
    weight_x = [
        go(to_kv(wg.at[b], wg.at[b], w_s.at[d], w_r.at[d], x_peer(d))) for d in (2, 1, 3)
    ]
    weight_own = go(to_kv(wg.at[b], wg.at[b], w_s.at[0], w_r.at[0], sibling))

    for copy in ids + a1:
        copy.wait_recv()
    lane_q = lax.broadcasted_iota(jnp.int32, (NB * pages, NZ * ROWS), 1)
    lane_request = (x * 128 + (lane_q // ROWS) * 16 + c * ROWS + lax.rem(lane_q, ROWS)).astype(F32)
    wanted = idc[...].reshape(NB * pages, 128)[:, : NZ * ROWS]
    pick = jnp.where(wanted == lane_request, 1.0, 0.0).astype(BF16)
    line = qz[...].astype(F32).reshape(NZ * ROWS, FEAT).astype(BF16)
    picked = jnp.dot(pick, line, preferred_element_type=F32)
    qs[...] = picked.reshape(NB, blocks, ROWS, FEAT).astype(BF16)
    a2 = [go(to_kv(qs.at[b_at(e)], qr.at[b], a2_s.at[e], a2_r.at[e], b_peer(e))) for e in FAR_FIRST]
    qr[b] = qs[b]
    loads[1].wait()
    loads[2].wait()
    for copy in a2:
        copy.wait_recv()

    lane24 = lax.broadcasted_iota(jnp.int32, (pages, 128), 1)
    tops = jnp.zeros((pages, 128), F32)
    for h in range(HEADS):
        head = slice(h * HD, (h + 1) * HD)
        query = jnp.sum(qr[:, :, :, head].astype(F32), axis=0).reshape(pages, HD).astype(BF16)
        score = SCALE * lax.dot_general(
            query, k_ref[:, head], (((1,), (1,)), ((), ())), preferred_element_type=F32
        )
        score = jnp.where(live, score, FLOOR)
        top = jnp.max(score, axis=1, keepdims=True)
        weight = jnp.where(live, jnp.exp(score - top), 0.0).astype(BF16)
        total = jnp.sum(weight.astype(F32), axis=1, keepdims=True)
        part = jnp.dot(weight, v_ref[:, head], preferred_element_type=F32) / total
        ob[b, :blocks, :, head] = part.reshape(blocks, ROWS, HD).astype(BF16)
        tops = jnp.where(lane24 == h, top + jnp.log(total), tops)
    request_high = jnp.floor(page_request * 0.125)
    stats = split3(tops)
    stats = jnp.where(lane24 == 24, request_high + 1.0, stats)
    stats = jnp.where(lane24 == 25, page_request - 8.0 * request_high, stats)
    ob[b, :blocks, :, FEAT:] = stats.reshape(blocks, ROWS, 128).astype(BF16)
    mine = ob.at[b, pl.ds(0, blocks)]
    b1 = [go(to_kv(mine, mine, b1_s.at[e], b1_r.at[e], b_peer(e))) for e in FAR_FIRST]
    for copy in b1:
        copy.wait_recv()

    depth = NB * ob.shape[1] * ROWS
    count = NZ * ROWS
    turned = ob[:, :, :, FEAT:].astype(F32).reshape(depth, 128).T
    row_top = turned[0:8] + turned[8:16] + turned[16:24]
    row_request = turned[24:25] * 8.0 + turned[25:26]
    row_q = lax.broadcasted_iota(jnp.int32, (count, depth), 0)
    my_request = (
        lax.rem(row_q // ROWS + 4, NZ) * 64 + b * ROWS + lax.rem(row_q, ROWS) + 8
    ).astype(F32)
    match = jnp.broadcast_to(row_request, (count, depth)) == my_request
    lane64 = lax.broadcasted_iota(jnp.int32, (count, 128), 1)
    tops = jnp.full((count, 128), FLOOR, F32)
    for h in range(HEADS):
        head = slice(h * HD, (h + 1) * HD)
        level = jnp.where(match, jnp.broadcast_to(row_top[h : h + 1], (count, depth)), FLOOR)
        top = jnp.max(level, axis=1, keepdims=True)
        weight = jnp.where(match, jnp.exp(level - top), 0.0).astype(BF16)
        total = jnp.sum(weight.astype(F32), axis=1, keepdims=True)
        rows = ob[:, :, :, head].astype(F32).reshape(depth, HD).astype(BF16)
        some = total > 0.0
        safe = jnp.where(some, total, 1.0)
        part = jnp.dot(weight, rows, preferred_element_type=F32) / safe
        cb[:, :, head] = part.reshape(NZ, ROWS, HD).astype(BF16)
        tops = jnp.where(lane64 == h, jnp.where(some, top + jnp.log(safe), FLOOR), tops)
    cb[:, :, FEAT:] = split3(tops).reshape(NZ, ROWS, 128).astype(BF16)
    b2 = [go(to_kv(cb.at[z_at(d)], rb.at[z], b2_s.at[d], b2_r.at[d], z_peer(d))) for d in FAR_FIRST]
    rb[z] = cb[z]

    weight_on = []
    for copy, d in zip(weight_x, (2, 1, 3)):
        copy.wait_recv()
        block = wg.at[lax.rem(x + NX - d, NX) * 2 + c]
        weight_on.append(go(to_kv(block, block, f_s.at[d], f_r.at[d], sibling)))

    for copy in b2:
        copy.wait_recv()
    self_copy.wait_recv()

    level = join3(rb[:, :, FEAT:].astype(F32))
    share = jnp.exp(level - jnp.max(level, axis=0, keepdims=True))
    share = share / jnp.sum(share, axis=0, keepdims=True)
    for h in range(HEADS):
        head = slice(h * HD, (h + 1) * HD)
        part = jnp.sum(share[:, :, h : h + 1] * rb[:, :, head].astype(F32), axis=0)
        az[z, :, head] = part.astype(BF16)
    b3 = [go(to_kv(az.at[z], az.at[z], b3_s.at[d], b3_r.at[d], z_peer(d))) for d in FAR_FIRST]
    weight_own.wait_recv()
    for copy in weight_on + b3:
        copy.wait_recv()

    attended = az[...].astype(F32).reshape(count, FEAT).astype(BF16)
    for block in range(NB):
        product = jnp.dot(attended, wg[block], preferred_element_type=F32)
        pc[:, :, block * 128 : (block + 1) * 128] = product.reshape(NZ, ROWS, 128).astype(BF16)

    def band_at(d):
        return lax.rem(t + d + 4, NT)

    c1 = [
        go(to_tp(pc.at[band_at(d)], cr.at[t], c1_s.at[d], c1_r.at[d], lax.rem(t + d, NT)))
        for d in FAR_FIRST
    ]
    cr[t] = pc[band_at(0)]
    for copy in c1:
        copy.wait_recv()
    summed = jnp.sum(cr[...].astype(F32), axis=0)
    for block in range(NB):
        fs[block] = summed[:, block * 128 : (block + 1) * 128]
    c2 = [go(to_kv(fs.at[b_at(e)], fr.at[b], c2_s.at[e], c2_r.at[e], b_peer(e))) for e in FAR_FIRST]
    fr[b] = fs[b]
    for copy in c2:
        copy.wait_recv()
    out_ref[...] = fr[...].reshape(NB * ROWS, 128)
    for copy in sends:
        copy.wait_send()


def on_device(
    queries,
    new_keys,
    new_values,
    keys,
    values,
    slot_request,
    slot_valid,
    out_weight,
    out_bias,
    residual,
):
    slots = keys.shape[0]
    depth, columns = out_weight.shape
    pages = slots // PAGE
    blocks = pages // ROWS
    padded = 4
    vmem = pl.BlockSpec(memory_space=pltpu.VMEM)
    hbm = pl.BlockSpec(memory_space=pl.ANY)
    dma = pltpu.SemaphoreType.DMA
    pairs = [dma((NB,))] * 2
    projected = pl.pallas_call(
        kernel,
        out_shape=jax.ShapeDtypeStruct((NB * ROWS, 128), F32),
        in_specs=[vmem] * 5 + [hbm] * 3,
        out_specs=vmem,
        scratch_shapes=[
            pltpu.VMEM((slots, FEAT), BF16),
            pltpu.VMEM((slots, FEAT), BF16),
            pltpu.VMEM((depth, columns), BF16),
            pltpu.VMEM((NB, depth, 128), BF16),
            pltpu.VMEM((NB, pages, 128), F32),
            pltpu.VMEM((NZ, ROWS, FEAT), BF16),
            pltpu.VMEM((NB, blocks, ROWS, FEAT), BF16),
            pltpu.VMEM((NB, blocks, ROWS, FEAT), BF16),
            pltpu.VMEM((NB, padded, ROWS, WIDE), BF16),
            pltpu.VMEM((NZ, ROWS, WIDE), BF16),
            pltpu.VMEM((NZ + 1, ROWS, WIDE), BF16),
            pltpu.VMEM((ROWS, WIDE), BF16),
            pltpu.VMEM((NZ, ROWS, FEAT), BF16),
            pltpu.VMEM((NZ, ROWS, NB * 128), BF16),
            pltpu.VMEM((NT, ROWS, NB * 128), BF16),
            pltpu.VMEM((NB, ROWS, 128), F32),
            pltpu.VMEM((NB, ROWS, 128), F32),
            dma((3,)),
            dma((NX,)), dma((NX,)), dma((NX,)), dma((NX,)),
        ]
        + pairs * 8
        + [dma, dma],
        compiler_params=pltpu.CompilerParams(
            collective_id=0, has_side_effects=True, vmem_limit_bytes=40 << 20
        ),
        name="paged_decode",
    )(
        queries, new_keys, new_values, slot_request.reshape(1, slots),
        slot_valid.reshape(1, slots), keys, values, out_weight,
    )
    total = (
        residual.astype(F32) + projected[:, :columns] + out_bias.astype(F32)[None, :]
    )
    return total.astype(BF16)


def solution(mesh):
    placed = (
        P("kv", "tp"),
        P("kv", "tp"),
        P("kv", "tp"),
        P("kv", "tp"),
        P("kv", "tp"),
        P("kv"),
        P("kv"),
        P("tp", "kv"),
        P("kv"),
        P("tp", "kv"),
    )
    return jax.shard_map(
        on_device, mesh=mesh, in_specs=placed, out_specs=P("tp", "kv"), check_vma=False
    )
```

time: 627 us -> 68.4 us (0.11)
  blocking collectives: 548 us -> 0 us
  Pallas kernels: 0 us -> 63.4 us
  waiting for transfers between devices: 32.5 us -> 0 us
  other arithmetic: 14.4 us -> 0.62 us
  between operations: 13.6 us -> 0.09 us
  local copies, waits for them, and re-layouts: 10.8 us -> 4.02 us
    psum x1 -> x0, blocking collectives: 246 us -> none  [on_device(): numer, denom = lax.psum((numer_local, denom_local), 'kv')]
    pmax x1 -> x0, blocking collectives: 243 us -> none  [on_device(): row_top = lax.pmax(local_top, 'kv')]
    pallas_call x0 -> x1, Pallas kernels: none -> 63.4 us  [on_device(): pl.pallas_call(kernel, out_shape=jax.ShapeDtypeStruct((NB * ROWS, 128), F...]
    all_gather x1 -> x0, blocking collectives: 58 us -> none  [on_device(): every_query = lax.all_gather(queries, 'kv', axis=0, tiled=True)]
    reduce_scatter x1 -> x0, waiting for transfers between devices: 32.4 us -> none  [on_device(): lax.psum_scatter(jnp.dot(attended, out_weight, preferred_element_type=jnp...]
    scatter-add x2 -> x0, other arithmetic: 8.14 us -> none  [the longest x1 4.88 us: on_device(): jax.ops.segment_sum(weighted.reshape(slot_count, head_count * HD), slot_r...]
  transfers between devices with their start and end apart: 2 -> 0, of which waited for: 1 -> 0; matrix products, arithmetic and copies ran while one was open for 1% -> 0% of each run, Pallas kernels for 0% -> 0%
where the time goes in v1:
time: 68.4 us; the launch traced here: 68.1 us
  Pallas kernels  63.4 us (93%)
  local copies, waits for them, and re-layouts  4.02 us (6%)
    pallas_call x1, Pallas kernels, on_device(): pl.pallas_call(kernel, out_shape=jax.ShapeDtypeStruct((NB * ROWS, 128), F...  63.4 us
    unnamed x19, local copies, waits for them, and re-layouts  4.02 us

profile of v1, /device:TPU:1, one launch (start us, length us, event | category | flops | bytes accessed | tf_op | source)
XLA Modules:
  0.0 68.1 jit_solution(5312514103280252308)
XLA Ops:
  0.0 0.0 copy-start.6
  0.0 0.0 copy-start.2
  0.0 0.0 copy-start.3
  0.0 0.0 copy-start.4
  0.0 1.1 %copy.11.w_hbm = bf16[896,112]{1,0:T(8,128)(2,1)S(1)} copy(bf16[896,112]{0,1:T(8,128)(2,1)} %param.17) | data formatting | bytes 401408 | tf_op args[7]
  1.2 0.0 copy-done.6
  1.2 0.0 copy-start.7
  1.2 0.7 copy-done.7
  1.9 0.0 copy-done.2
  1.9 0.0 copy-done.3
  1.9 0.0 copy-done.4
  1.9 0.0 copy-start
  1.9 1.1 %copy-done = bf16[384,896]{1,0:T(8,128)(2,1)S(1)} copy-done((bf16[384,896]{1,0:T(8,128)(2,1)S(1)}, bf16[384,896]{1,0:T(8,128)(2,1)}, u32[]{:S(2)}) %copy-start) | copy-done | bytes 688152
  3.0 0.0 copy-start.1
  3.0 1.1 %copy-done.1 = bf16[384,896]{1,0:T(8,128)(2,1)S(1)} copy-done((bf16[384,896]{1,0:T(8,128)(2,1)S(1)}, bf16[384,896]{1,0:T(8,128)(2,1)}, u32[]{:S(2)}) %copy-start.1) | copy-done | bytes 688152
  4.1 0.0 copy-start.8
  4.1 0.0 copy-start.5
  4.1 63.4 %paged_decode.1 = f32[64,128]{1,0:T(8,128)S(1)} custom-call(bf16[8,896]{1,0:T(8,128)(2,1)S(1)} %copy-done.2, bf16[8,896]{1,0:T(8,128)(2,1)S(1)} %copy-done.3, bf16[8,896]{1,0:T(8,128)(2,1)S(1)} %copy-done.4, s32[1,384]{1,0:T(1,128)S(1)} %reshape.7.sr_ref, s32[1,384]{1,0:T(1,128)S(1)} %reshape.8.sv_ref, bf16[384,896]{1,0:T(8,128)(2,1)S(1)} %copy-done, ...), custom_call_target="tpu_custom_call" | custom-call | tf_op jit(solution)/shard_map/paged_decode/pallas_call | solution.py:290
  67.5 0.0 copy-done.8
  67.5 0.0 copy-done.5
  67.5 0.6 add_convert_fusion
  (3 shorter events, 0.0 us)
Async XLA Ops:
  0.0 1.2 %copy-start.6 = (s32[384]{0:T(512)S(1)}, s32[384]{0:T(512)}, u32[]{:S(2)}) copy-start(s32[384]{0:T(512)} %param.15) | copy-start | bytes 4612
  0.0 1.9 %copy-start.2 = (bf16[8,896]{1,0:T(8,128)(2,1)S(1)}, bf16[8,896]{1,0:T(8,128)(2,1)}, u32[]{:S(2)}) copy-start(bf16[8,896]{1,0:T(8,128)(2,1)} %q_ref.1) | copy-start | bytes 43012
  0.0 1.9 %copy-start.3 = (bf16[8,896]{1,0:T(8,128)(2,1)S(1)}, bf16[8,896]{1,0:T(8,128)(2,1)}, u32[]{:S(2)}) copy-start(bf16[8,896]{1,0:T(8,128)(2,1)} %nk_ref.1) | copy-start | bytes 43012
  0.0 1.9 %copy-start.4 = (bf16[8,896]{1,0:T(8,128)(2,1)S(1)}, bf16[8,896]{1,0:T(8,128)(2,1)}, u32[]{:S(2)}) copy-start(bf16[8,896]{1,0:T(8,128)(2,1)} %nv_ref.1) | copy-start | bytes 43012
  1.2 0.7 %copy-start.7 = (s32[384]{0:T(512)S(1)}, s32[384]{0:T(512)}, u32[]{:S(2)}) copy-start(s32[384]{0:T(512)} %param.16) | copy-start | bytes 4612
  1.9 1.1 %copy-start = (bf16[384,896]{1,0:T(8,128)(2,1)S(1)}, bf16[384,896]{1,0:T(8,128)(2,1)}, u32[]{:S(2)}) copy-start(bf16[384,896]{1,0:T(8,128)(2,1)} %k_hbm.1) | copy-start | bytes 2064388
  3.0 1.1 %copy-start.1 = (bf16[384,896]{1,0:T(8,128)(2,1)S(1)}, bf16[384,896]{1,0:T(8,128)(2,1)}, u32[]{:S(2)}) copy-start(bf16[384,896]{1,0:T(8,128)(2,1)} %v_hbm.1) | copy-start | bytes 2064388
  4.1 63.4 %copy-start.8 = (bf16[112]{0:T(256)(128)(2,1)S(1)}, bf16[112]{0:T(256)(128)(2,1)}, u32[]{:S(2)}) copy-start(bf16[112]{0:T(256)(128)(2,1)} %param.18) | copy-start | bytes 676
  4.1 63.4 %copy-start.5 = (bf16[64,112]{1,0:T(8,128)(2,1)S(1)}, bf16[64,112]{1,0:T(8,128)(2,1)}, u32[]{:S(2)}) copy-start(bf16[64,112]{1,0:T(8,128)(2,1)} %param.19) | copy-start | bytes 43012

commit v2 on v1

--- a/solution.py
+++ b/solution.py
@@ -21,6 +21,8 @@
 
 FAR_FIRST = (4, 3, 5, 2, 6, 1, 7)
 
+EARLY = 2
+
 
 def kv_of(x, z, c):
     return (x * NZ + z) * 2 + c
@@ -41,10 +43,10 @@
 
 
 def kernel(
-    q_ref, nk_ref, nv_ref, sr_ref, sv_ref, k_hbm, v_hbm, w_hbm, out_ref,
-    k_ref, v_ref, w_ref, wg, idc, qz, qs, qr, ob, cb, rb, sb, az, pc, cr, fs, fr,
+    q_hbm, nk_hbm, nv_hbm, sr_hbm, sv_hbm, k_hbm, v_hbm, w_hbm, out_ref,
+    nk_ref, nv_ref, sr_ref, sv_ref, k_ref, v_ref, wg, idc, qz, qs, qr, ob, cb, rb, sb, az, pc, fr,
     local, w_s, w_r, f_s, f_r, id_s, id_r, a1_s, a1_r, a2_s, a2_r, b1_s, b1_r, b2_s, b2_r,
-    b3_s, b3_r, c1_s, c1_r, c2_s, c2_r, self_s, self_r,
+    b3_s, b3_r, c1_s, c1_r, self_s, self_r,
 ):
     k = lax.axis_index("kv")
     t = lax.axis_index("tp")
@@ -84,16 +86,6 @@
 
     sibling = kv_of(x, z, 1 - c)
     owner = kv_of(lax.rem(z, 4), lax.rem(2 * x + z // 4 + 4, NZ), c)
-    band = lax.rem(z + 4, NZ)
-    home = kv_of(band // 2, lax.rem(band, 2) * 4 + x, c)
-
-    loads = [
-        pltpu.make_async_copy(w_hbm, w_ref, local.at[0]),
-        pltpu.make_async_copy(k_hbm, k_ref, local.at[1]),
-        pltpu.make_async_copy(v_hbm, v_ref, local.at[2]),
-    ]
-    for load in loads:
-        load.start()
 
     barrier = pltpu.get_barrier_semaphore()
     for d in range(1, 8):
@@ -102,54 +94,84 @@
         pl.semaphore_signal(
             barrier, inc=1, device_id={"tp": lax.rem(t + d, NT)}, device_id_type=MESH
         )
-    pl.semaphore_signal(barrier, inc=1, device_id={"kv": owner}, device_id_type=MESH)
-    pl.semaphore_signal(barrier, inc=1, device_id={"kv": home}, device_id_type=MESH)
+
+    small = [
+        pltpu.make_async_copy(sr_hbm, sr_ref, local.at[1]),
+        pltpu.make_async_copy(sv_hbm, sv_ref, local.at[2]),
+        pltpu.make_async_copy(q_hbm, qz.at[z], local.at[0]),
+        pltpu.make_async_copy(nk_hbm, nk_ref, local.at[3]),
+        pltpu.make_async_copy(nv_hbm, nv_ref, local.at[4]),
+    ]
+    large = [
+        pltpu.make_async_copy(w_hbm, wg.at[b], local.at[5]),
+        pltpu.make_async_copy(k_hbm, k_ref, local.at[6]),
+        pltpu.make_async_copy(v_hbm, v_ref, local.at[7]),
+    ]
+    for load in small + large:
+        load.start()
+
+    sends = []
+
+    def go(copy):
+        copy.start()
+        sends.append(copy)
+        return copy
+
+    def arrive(*copies):
+        for copy in copies:
+            copy.wait_recv()
 
     slots = k_ref.shape[0]
     pages = slots // PAGE
     blocks = pages // ROWS
     lane_page = lax.broadcasted_iota(jnp.int32, (pages, slots), 1) // PAGE
     on_page = lane_page == lax.broadcasted_iota(jnp.int32, (pages, slots), 0)
-    request_row = jnp.broadcast_to(sr_ref[...].astype(F32), (pages, slots))
+    small[0].wait()
+    request_row = jnp.broadcast_to(sr_ref[...].reshape(1, slots).astype(F32), (pages, slots))
     page_request = jnp.max(jnp.where(on_page, request_row, -1.0), axis=1, keepdims=True)
-    live = jnp.where(on_page, jnp.broadcast_to(sv_ref[...], (pages, slots)), 0) == 1
     idc[b] = jnp.broadcast_to(page_request, (pages, 128))
-
+    pl.semaphore_wait(barrier, 21)
+
+    a1 = [go(to_kv(q_hbm, qz.at[z], a1_s.at[d], a1_r.at[d], z_peer(d))) for d in FAR_FIRST]
+    ids = [go(to_kv(idc.at[b], idc.at[b], id_s.at[e], id_r.at[e], b_peer(e))) for e in FAR_FIRST]
+
+    def weights_x(first, last):
+        part = pl.ds(first, last - first)
+        sem = 0 if first == 0 else NX
+        return [
+            go(to_kv(w_hbm.at[part], wg.at[b, part], w_s.at[sem + d], w_r.at[sem + d], x_peer(d)))
+            for d in (2, 1, 3)
+        ]
+
+    def weights_on(copies, first, last):
+        part = pl.ds(first, last - first)
+        sem = 0 if first == 0 else NX
+        done = []
+        for copy, d in zip(copies, (2, 1, 3)):
+            arrive(copy)
+            block = wg.at[lax.rem(x + NX - d, NX) * 2 + c, part]
+            done.append(go(to_kv(block, block, f_s.at[sem + d], f_r.at[sem + d], sibling)))
+        return done
+
+    chunks = wg.shape[1]
+    early = weights_x(0, EARLY)
+    weight_own = go(to_kv(w_hbm, wg.at[b], w_s.at[0], w_r.at[0], sibling))
+
+    for load in small[1:]:
+        load.wait()
+    live_row = jnp.broadcast_to(sv_ref[...].reshape(1, slots), (pages, slots))
+    live = jnp.where(on_page, live_row, 0) == 1
     lane8 = lax.broadcasted_iota(jnp.int32, (ROWS, 128), 1)
     own = jnp.zeros((ROWS, 128), F32)
     for h in range(HEADS):
         head = slice(h * HD, (h + 1) * HD)
-        product = q_ref[:, head].astype(F32) * nk_ref[:, head].astype(F32)
+        product = qz[z, :, head].astype(F32) * nk_ref[:, head].astype(F32)
         own = jnp.where(lane8 == h, jnp.sum(product, axis=1, keepdims=True) * SCALE, own)
     sb[:, :FEAT] = nv_ref[...]
     sb[:, FEAT:] = split3(own).astype(BF16)
-
-    qz[z] = q_ref[...]
     ob[:, blocks:] = jnp.zeros((NB, ob.shape[1] - blocks, ROWS, WIDE), BF16)
 
-    pl.semaphore_wait(barrier, 23)
-
-    sends = []
-
-    def go(copy):
-        copy.start()
-        sends.append(copy)
-        return copy
-
-    a1 = [go(to_kv(q_ref, qz.at[z], a1_s.at[d], a1_r.at[d], z_peer(d))) for d in FAR_FIRST]
-    ids = [go(to_kv(idc.at[b], idc.at[b], id_s.at[e], id_r.at[e], b_peer(e))) for e in FAR_FIRST]
-    self_copy = go(to_kv(sb, rb.at[NZ], self_s, self_r, owner))
-    loads[0].wait()
-    columns = w_ref.shape[1]
-    wg[b, :, :columns] = w_ref[...]
-    wg[b, :, columns:] = jnp.zeros((w_ref.shape[0], 128 - columns), BF16)
-    weight_x = [
-        go(to_kv(wg.at[b], wg.at[b], w_s.at[d], w_r.at[d], x_peer(d))) for d in (2, 1, 3)
-    ]
-    weight_own = go(to_kv(wg.at[b], wg.at[b], w_s.at[0], w_r.at[0], sibling))
-
-    for copy in ids + a1:
-        copy.wait_recv()
+    arrive(*ids, *a1)
     lane_q = lax.broadcasted_iota(jnp.int32, (NB * pages, NZ * ROWS), 1)
     lane_request = (x * 128 + (lane_q // ROWS) * 16 + c * ROWS + lax.rem(lane_q, ROWS)).astype(F32)
     wanted = idc[...].reshape(NB * pages, 128)[:, : NZ * ROWS]
@@ -159,10 +181,11 @@
     qs[...] = picked.reshape(NB, blocks, ROWS, FEAT).astype(BF16)
     a2 = [go(to_kv(qs.at[b_at(e)], qr.at[b], a2_s.at[e], a2_r.at[e], b_peer(e))) for e in FAR_FIRST]
     qr[b] = qs[b]
-    loads[1].wait()
-    loads[2].wait()
-    for copy in a2:
-        copy.wait_recv()
+    large[1].wait()
+    large[2].wait()
+    arrive(*a2)
+    self_copy = go(to_kv(sb, rb.at[NZ], self_s, self_r, owner))
+    early_on = weights_on(early, 0, EARLY)
 
     lane24 = lax.broadcasted_iota(jnp.int32, (pages, 128), 1)
     tops = jnp.zeros((pages, 128), F32)
@@ -186,8 +209,8 @@
     ob[b, :blocks, :, FEAT:] = stats.reshape(blocks, ROWS, 128).astype(BF16)
     mine = ob.at[b, pl.ds(0, blocks)]
     b1 = [go(to_kv(mine, mine, b1_s.at[e], b1_r.at[e], b_peer(e))) for e in FAR_FIRST]
-    for copy in b1:
-        copy.wait_recv()
+    arrive(*b1)
+    late = weights_x(EARLY, chunks)
 
     depth = NB * ob.shape[1] * ROWS
     count = NZ * ROWS
@@ -217,15 +240,7 @@
     b2 = [go(to_kv(cb.at[z_at(d)], rb.at[z], b2_s.at[d], b2_r.at[d], z_peer(d))) for d in FAR_FIRST]
     rb[z] = cb[z]
 
-    weight_on = []
-    for copy, d in zip(weight_x, (2, 1, 3)):
-        copy.wait_recv()
-        block = wg.at[lax.rem(x + NX - d, NX) * 2 + c]
-        weight_on.append(go(to_kv(block, block, f_s.at[d], f_r.at[d], sibling)))
-
-    for copy in b2:
-        copy.wait_recv()
-    self_copy.wait_recv()
+    arrive(*b2, self_copy)
 
     level = join3(rb[:, :, FEAT:].astype(F32))
     share = jnp.exp(level - jnp.max(level, axis=0, keepdims=True))
@@ -235,33 +250,38 @@
         part = jnp.sum(share[:, :, h : h + 1] * rb[:, :, head].astype(F32), axis=0)
         az[z, :, head] = part.astype(BF16)
     b3 = [go(to_kv(az.at[z], az.at[z], b3_s.at[d], b3_r.at[d], z_peer(d))) for d in FAR_FIRST]
-    weight_own.wait_recv()
-    for copy in weight_on + b3:
-        copy.wait_recv()
+    late_on = weights_on(late, EARLY, chunks)
+    arrive(*b3)
+    arrive(weight_own, *early_on, *late_on)
+    large[0].wait()
 
     attended = az[...].astype(F32).reshape(count, FEAT).astype(BF16)
-    for block in range(NB):
-        product = jnp.dot(attended, wg[block], preferred_element_type=F32)
-        pc[:, :, block * 128 : (block + 1) * 128] = product.reshape(NZ, ROWS, 128).astype(BF16)
-
-    def band_at(d):
-        return lax.rem(t + d + 4, NT)
-
-    c1 = [
-        go(to_tp(pc.at[band_at(d)], cr.at[t], c1_s.at[d], c1_r.at[d], lax.rem(t + d, NT)))
-        for d in FAR_FIRST
-    ]
-    cr[t] = pc[band_at(0)]
-    for copy in c1:
-        copy.wait_recv()
-    summed = jnp.sum(cr[...].astype(F32), axis=0)
-    for block in range(NB):
-        fs[block] = summed[:, block * 128 : (block + 1) * 128]
-    c2 = [go(to_kv(fs.at[b_at(e)], fr.at[b], c2_s.at[e], c2_r.at[e], b_peer(e))) for e in FAR_FIRST]
-    fr[b] = fs[b]
-    for copy in c2:
-        copy.wait_recv()
-    out_ref[...] = fr[...].reshape(NB * ROWS, 128)
+    columns = chunks * 16
+    c1 = []
+    for e in FAR_FIRST + (0,):
+        product = lax.dot_general(
+            attended, wg[b_at(e)].reshape(columns, FEAT), (((1,), (1,)), ((), ())),
+            preferred_element_type=F32,
+        )
+        pc[e, :, :, :columns] = product.reshape(NZ, ROWS, columns).astype(BF16)
+        for d in FAR_FIRST + (0,):
+            rows = lax.rem(t + d + 4, NT)
+            if d == 0 and e == 0:
+                fr[t * NB + b] = pc[e, rows]
+                continue
+            sem = d * NB + e
+            c1.append(
+                go(
+                    pltpu.make_async_remote_copy(
+                        src_ref=pc.at[e, rows], dst_ref=fr.at[t * NB + b],
+                        send_sem=c1_s.at[sem], recv_sem=c1_r.at[sem],
+                        device_id={"kv": b_peer(e), "tp": lax.rem(t + d, NT)},
+                        device_id_type=MESH,
+                    )
+                )
+            )
+    arrive(*c1)
+    out_ref[...] = jnp.sum(fr[...].astype(F32).reshape(NT, NB * ROWS, 128), axis=0)
     for copy in sends:
         copy.wait_send()
 
@@ -279,24 +299,27 @@
     residual,
 ):
     slots = keys.shape[0]
-    depth, columns = out_weight.shape
+    columns = out_weight.shape[1]
     pages = slots // PAGE
     blocks = pages // ROWS
     padded = 4
     vmem = pl.BlockSpec(memory_space=pltpu.VMEM)
-    hbm = pl.BlockSpec(memory_space=pl.ANY)
+    hbm = pl.BlockSpec(memory_space=pltpu.HBM)
     dma = pltpu.SemaphoreType.DMA
     pairs = [dma((NB,))] * 2
     projected = pl.pallas_call(
         kernel,
         out_shape=jax.ShapeDtypeStruct((NB * ROWS, 128), F32),
-        in_specs=[vmem] * 5 + [hbm] * 3,
+        in_specs=[hbm] * 8,
         out_specs=vmem,
         scratch_shapes=[
+            pltpu.VMEM((ROWS, FEAT), BF16),
+            pltpu.VMEM((ROWS, FEAT), BF16),
+            pltpu.VMEM((slots,), jnp.int32),
+            pltpu.VMEM((slots,), jnp.int32),
             pltpu.VMEM((slots, FEAT), BF16),
             pltpu.VMEM((slots, FEAT), BF16),
-            pltpu.VMEM((depth, columns), BF16),
-            pltpu.VMEM((NB, depth, 128), BF16),
+            pltpu.VMEM((NB, columns // 16, 16, FEAT), BF16),
             pltpu.VMEM((NB, pages, 128), F32),
             pltpu.VMEM((NZ, ROWS, FEAT), BF16),
             pltpu.VMEM((NB, blocks, ROWS, FEAT), BF16),
@@ -306,22 +329,20 @@
             pltpu.VMEM((NZ + 1, ROWS, WIDE), BF16),
             pltpu.VMEM((ROWS, WIDE), BF16),
             pltpu.VMEM((NZ, ROWS, FEAT), BF16),
-            pltpu.VMEM((NZ, ROWS, NB * 128), BF16),
-            pltpu.VMEM((NT, ROWS, NB * 128), BF16),
-            pltpu.VMEM((NB, ROWS, 128), F32),
-            pltpu.VMEM((NB, ROWS, 128), F32),
-            dma((3,)),
-            dma((NX,)), dma((NX,)), dma((NX,)), dma((NX,)),
+            pltpu.VMEM((NB, NZ, ROWS, 128), BF16),
+            pltpu.VMEM((NT * NB, ROWS, 128), BF16),
+            dma((8,)),
+            dma((2 * NX,)), dma((2 * NX,)), dma((2 * NX,)), dma((2 * NX,)),
         ]
-        + pairs * 8
-        + [dma, dma],
+        + pairs * 6
+        + [dma((NT * NB,)), dma((NT * NB,)), dma, dma],
         compiler_params=pltpu.CompilerParams(
-            collective_id=0, has_side_effects=True, vmem_limit_bytes=40 << 20
+            collective_id=0, has_side_effects=True, vmem_limit_bytes=63 << 20
         ),
         name="paged_decode",
     )(
-        queries, new_keys, new_values, slot_request.reshape(1, slots),
-        slot_valid.reshape(1, slots), keys, values, out_weight,
+        queries, new_keys, new_values, slot_request, slot_valid, keys, values,
+        out_weight.T.reshape(columns // 16, 16, FEAT),
     )
     total = (
         residual.astype(F32) + projected[:, :columns] + out_bias.astype(F32)[None, :]

time: 68.4 us -> 58 us (0.85)
  Pallas kernels: 63.4 us -> 55.7 us
  local copies, waits for them, and re-layouts: 4.02 us -> 0.66 us
  other arithmetic: 0.62 us -> 1.37 us
    pallas_call x1, Pallas kernels: 63.4 us -> 55.7 us  [on_device(): pl.pallas_call(kernel, out_shape=jax.ShapeDtypeStruct((NB * ROWS, 128), F...]
    unnamed x19 -> x4, local copies, waits for them, and re-layouts: 4.02 us -> 0.66 us
    convert_element_type x1, other arithmetic: 0.61 us -> 1.37 us  [on_device(): return total.astype(BF16)]
where the time goes in v2:
time: 58 us; the launch traced here: 57.7 us
  Pallas kernels  55.7 us (96%)
  other arithmetic  1.37 us (2%)
  local copies, waits for them, and re-layouts  0.66 us (1%)
    pallas_call x1, Pallas kernels, on_device(): pl.pallas_call(kernel, out_shape=jax.ShapeDtypeStruct((NB * ROWS, 128), F...  55.7 us
    convert_element_type x1, other arithmetic, on_device(): return total.astype(BF16)  1.37 us

profile of v2, /device:TPU:1, one launch (start us, length us, event | category | flops | bytes accessed | tf_op | source)
XLA Modules:
  0.0 57.7 jit_solution(10143505536333276837)
XLA Ops:
  0.0 0.0 copy-start.1
  0.0 0.7 %copy-done.1 = bf16[112]{0:T(256)(128)(2,1)S(1)} copy-done((bf16[112]{0:T(256)(128)(2,1)S(1)}, bf16[112]{0:T(256)(128)(2,1)}, u32[]{:S(2)}) %copy-start.1) | copy-done | bytes 248
  0.7 0.0 copy-start
  0.7 55.7 %paged_decode.1 = f32[64,128]{1,0:T(8,128)} custom-call(bf16[8,896]{1,0:T(8,128)(2,1)} %q_hbm.1, bf16[8,896]{1,0:T(8,128)(2,1)} %nk_hbm.1, bf16[8,896]{1,0:T(8,128)(2,1)} %nv_hbm.1, s32[384]{0:T(512)} %sr_hbm.1, s32[384]{0:T(512)} %sv_hbm.1, bf16[384,896]{1,0:T(8,128)(2,1)} %k_hbm.1, bf16[384,896]{1,0:T(8,128)(2,1)} %v_hbm.1, bf16[7,16,896]{2,1,0:T(8,128)(2,1)} %bitcast.3), custom_call_target="tpu_custom_call" | custom-call | tf_op jit(solution)/shard_map/paged_decode/pallas_call | solution.py:310
  56.3 0.0 copy-done
  56.4 1.4 %add_convert_fusion = bf16[64,112]{1,0:T(8,128)(2,1)} fusion(f32[64,128]{1,0:T(8,128)} %paged_decode.1, bf16[64,112]{1,0:T(8,128)(2,1)S(1)} %copy-done, f32[112]{0:T(128)S(1)} %convert_element_type.10), kind=kLoop, calls=%fused_computation | loop fusion | flops 28672 | bytes 57792 | tf_op jit(solution)/shard_map/convert_element_type | solution.py:350
  (1 shorter events, 0.0 us)
Async XLA Ops:
  0.0 0.7 %copy-start.1 = (bf16[112]{0:T(256)(128)(2,1)S(1)}, bf16[112]{0:T(256)(128)(2,1)}, u32[]{:S(2)}) copy-start(bf16[112]{0:T(256)(128)(2,1)} %param.18) | copy-start | bytes 676
  0.7 55.7 %copy-start = (bf16[64,112]{1,0:T(8,128)(2,1)S(1)}, bf16[64,112]{1,0:T(8,128)(2,1)}, u32[]{:S(2)}) copy-start(bf16[64,112]{1,0:T(8,128)(2,1)} %param.19) | copy-start | bytes 43012

commit v3 on v2

v3 whole, which is shorter than its diff:
```python
import math

import jax
import jax.numpy as jnp
from jax import lax
from jax.experimental import pallas as pl
from jax.experimental.pallas import tpu as pltpu
from jax.sharding import PartitionSpec as P

HD = 128
HEADS = 7
FEAT = HEADS * HD
PAGE = 16
NX, NZ, NT, NB = 4, 8, 8, 8
ROWS = 8
FLOOR = -1e30
SCALE = 1.0 / math.sqrt(HD)
MESH = pl.DeviceIdType.MESH
F32, BF16 = jnp.float32, jnp.bfloat16

GROUPS = ((0, 4), (4, 3))

FAR_FIRST = (4, 3, 5, 2, 6, 1, 7)

EARLY = 3

GRANT = 63 << 20


def kv_of(x, z, c):
    return (x * NZ + z) * 2 + c


def head_at(h):
    return slice(h * HD, (h + 1) * HD)


def split3(tile):
    lane = lax.broadcasted_iota(jnp.int32, tile.shape, 1)
    tile = jnp.where(lane < 8, tile, 0.0)
    high = tile.astype(BF16).astype(F32)
    middle = (tile - high).astype(BF16).astype(F32)
    low = tile - high - middle
    return high + pltpu.roll(middle, 8, 1) + pltpu.roll(low, 16, 1)


def join3(tile):
    axis = tile.ndim - 1
    return tile + pltpu.roll(tile, 128 - 8, axis) + pltpu.roll(tile, 128 - 16, axis)


def kernel(
    q_hbm, nk_hbm, nv_hbm, sr_hbm, sv_hbm, k_hbm, v_hbm, w_hbm, out_ref,
    nk_ref, nv_ref, sr_ref, sv_ref, k_ref, v_ref, wg, idc, qz, qs, qr, ob, cb, rb, sb, az,
    acc, pc, fr, local, w_s, w_r, f_s, f_r, id_s, id_r, a1_s, a1_r, a2_s, a2_r, b1_s, b1_r,
    b2_s, b2_r, b3_s, b3_r, self_s, self_r, c_s, c_r,
):
    k = lax.axis_index("kv")
    t = lax.axis_index("tp")
    c = lax.rem(k, 2)
    xz = k // 2
    x = xz // NZ
    z = lax.rem(xz, NZ)
    b = x * 2 + c

    def to_kv(src, dst, send, recv, kv):
        return pltpu.make_async_remote_copy(
            src_ref=src, dst_ref=dst, send_sem=send, recv_sem=recv,
            device_id={"kv": kv}, device_id_type=MESH,
        )

    def z_at(d):
        return lax.rem(z + d, NZ)

    def b_at(e):
        return lax.rem(b + e, NB)

    def z_peer(d):
        return kv_of(x, z_at(d), c)

    def b_peer(e):
        other = b_at(e)
        return kv_of(other // 2, z, lax.rem(other, 2))

    def x_peer(d):
        return kv_of(lax.rem(x + d, NX), z, c)

    sibling = kv_of(x, z, 1 - c)
    owner = kv_of(lax.rem(z, 4), lax.rem(2 * x + z // 4 + 4, NZ), c)

    barrier = pltpu.get_barrier_semaphore()
    for d in range(1, 8):
        pl.semaphore_signal(barrier, inc=1, device_id={"kv": z_peer(d)}, device_id_type=MESH)
    for d in range(1, 8):
        pl.semaphore_signal(barrier, inc=1, device_id={"kv": b_peer(d)}, device_id_type=MESH)
    for d in range(1, 8):
        pl.semaphore_signal(
            barrier, inc=1, device_id={"tp": lax.rem(t + d, NT)}, device_id_type=MESH
        )

    def feats(g):
        first, heads = GROUPS[g]
        return pl.ds(first * HD, heads * HD)

    groups = range(len(GROUPS))
    small = [
        pltpu.make_async_copy(sr_hbm, sr_ref, local.at[0]),
        pltpu.make_async_copy(sv_hbm, sv_ref, local.at[1]),
        pltpu.make_async_copy(nk_hbm, nk_ref, local.at[2]),
        pltpu.make_async_copy(nv_hbm, nv_ref, local.at[3]),
    ] + [
        pltpu.make_async_copy(q_hbm.at[:, feats(g)], qz[g].at[z], local.at[4 + g]) for g in groups
    ]
    large = [
        pltpu.make_async_copy(w_hbm, wg.at[b], local.at[6]),
        pltpu.make_async_copy(k_hbm, k_ref, local.at[7]),
        pltpu.make_async_copy(v_hbm, v_ref, local.at[8]),
    ]
    for load in small:
        load.start()

    sends = []

    def go(copy):
        copy.start()
        sends.append(copy)
        return copy

    def arrive(*copies):
        for copy in copies:
            copy.wait_recv()

    pl.semaphore_wait(barrier, 21)

    a1 = [
        [
            go(
                to_kv(
                    q_hbm.at[:, feats(g)], qz[g].at[z], a1_s.at[g * 8 + d], a1_r.at[g * 8 + d],
                    z_peer(d),
                )
            )
            for d in FAR_FIRST
        ]
        for g in groups
    ]

    slots = k_ref.shape[0]
    pages = slots // PAGE
    blocks = pages // ROWS
    lane_page = lax.broadcasted_iota(jnp.int32, (pages, slots), 1) // PAGE
    on_page = lane_page == lax.broadcasted_iota(jnp.int32, (pages, slots), 0)
    small[0].wait()
    request_row = jnp.broadcast_to(sr_ref[...].reshape(1, slots).astype(F32), (pages, slots))
    page_request = jnp.max(jnp.where(on_page, request_row, -1.0), axis=1, keepdims=True)
    idc[b] = jnp.broadcast_to(page_request, (pages, 128))
    ids = [go(to_kv(idc.at[b], idc.at[b], id_s.at[e], id_r.at[e], b_peer(e))) for e in FAR_FIRST]

    for load in large:
        load.start()

    def weights_x(first, last):
        part = pl.ds(first, last - first)
        sem = 0 if first == 0 else NX
        return [
            go(to_kv(w_hbm.at[part], wg.at[b, part], w_s.at[sem + d], w_r.at[sem + d], x_peer(d)))
            for d in (2, 1, 3)
        ]

    def weights_on(copies, first, last):
        part = pl.ds(first, last - first)
        sem = 0 if first == 0 else NX
        done = []
        for copy, d in zip(copies, (2, 1, 3)):
            arrive(copy)
            block = wg.at[lax.rem(x + NX - d, NX) * 2 + c, part]
            done.append(go(to_kv(block, block, f_s.at[sem + d], f_r.at[sem + d], sibling)))
        return done

    chunks = wg.shape[1]
    early = weights_x(0, EARLY)
    weight_own = go(to_kv(w_hbm, wg.at[b], w_s.at[0], w_r.at[0], sibling))

    for load in small[1:]:
        load.wait()
    live_row = jnp.broadcast_to(sv_ref[...].reshape(1, slots), (pages, slots))
    live = jnp.where(on_page, live_row, 0) == 1
    lane8 = lax.broadcasted_iota(jnp.int32, (ROWS, 128), 1)
    for g, (first, heads) in enumerate(GROUPS):
        own = jnp.zeros((ROWS, 128), F32)
        for h in range(heads):
            new_key = nk_ref[:, head_at(first + h)].astype(F32)
            product = qz[g][z, :, head_at(h)].astype(F32) * new_key
            own = jnp.where(lane8 == h, jnp.sum(product, axis=1, keepdims=True) * SCALE, own)
        sb[g][:, : heads * HD] = nv_ref[:, feats(g)]
        sb[g][:, heads * HD :] = split3(own).astype(BF16)
        ob[g][:, blocks:] = jnp.zeros((NB, ob[g].shape[1] - blocks) + ob[g].shape[2:], BF16)

    a2 = []
    for g, (first, heads) in enumerate(GROUPS):
        if g == 0:
            arrive(*ids)
            lane_q = lax.broadcasted_iota(jnp.int32, (NB * pages, NZ * ROWS), 1)
            place = (lane_q // ROWS) * 16 + lax.rem(lane_q, ROWS)
            lane_request = (x * 128 + c * ROWS + place).astype(F32)
            wanted = idc[...].reshape(NB * pages, 128)[:, : NZ * ROWS]
            pick = jnp.where(wanted == lane_request, 1.0, 0.0).astype(BF16)
        arrive(*a1[g])
        line = qz[g][...].astype(F32).reshape(NZ * ROWS, heads * HD).astype(BF16)
        picked = jnp.dot(pick, line, preferred_element_type=F32)
        qs[g][...] = picked.reshape(NB, blocks, ROWS, heads * HD).astype(BF16)
        a2.append(
            [
                go(
                    to_kv(
                        qs[g].at[b_at(e)], qr[g].at[b], a2_s.at[g * 8 + e], a2_r.at[g * 8 + e],
                        b_peer(e),
                    )
                )
                for e in FAR_FIRST
            ]
        )
        qr[g][b] = qs[g][b]

    large[1].wait()
    large[2].wait()
    lane24 = lax.broadcasted_iota(jnp.int32, (pages, 128), 1)
    b1 = []
    for g, (first, heads) in enumerate(GROUPS):
        arrive(*a2[g])
        queries = jnp.sum(qr[g][...].astype(F32), axis=0).reshape(pages, heads * HD).astype(BF16)
        scores = [
            lax.dot_general(
                queries[:, head_at(h)], k_ref[:, head_at(first + h)], (((1,), (1,)), ((), ())),
                preferred_element_type=F32,
            )
            for h in range(heads)
        ]
        scores = [jnp.where(live, SCALE * score, FLOOR) for score in scores]
        top = [jnp.max(score, axis=1, keepdims=True) for score in scores]
        weights = [
            jnp.where(live, jnp.exp(score - high), 0.0).astype(BF16)
            for score, high in zip(scores, top)
        ]
        total = [jnp.sum(weight.astype(F32), axis=1, keepdims=True) for weight in weights]
        parts = [
            jnp.dot(weights[h], v_ref[:, head_at(first + h)], preferred_element_type=F32)
            for h in range(heads)
        ]
        tops = jnp.zeros((pages, 128), F32)
        for h in range(heads):
            part = (parts[h] / total[h]).reshape(blocks, ROWS, HD)
            ob[g][b, :blocks, :, head_at(h)] = part.astype(BF16)
            tops = jnp.where(lane24 == h, top[h] + jnp.log(total[h]), tops)
        stats = split3(tops)
        if g == 0:
            request_high = jnp.floor(page_request * 0.125)
            stats = jnp.where(lane24 == 24, request_high + 1.0, stats)
            stats = jnp.where(lane24 == 25, page_request - 8.0 * request_high, stats)
        stats = stats.reshape(blocks, ROWS, 128).astype(BF16)
        ob[g][b, :blocks, :, heads * HD :] = stats
        mine = ob[g].at[b, pl.ds(0, blocks)]
        b1.append(
            [
                go(to_kv(mine, mine, b1_s.at[g * 8 + e], b1_r.at[g * 8 + e], b_peer(e)))
                for e in FAR_FIRST
            ]
        )
    self_copies = [
        go(to_kv(sb[g], rb[g].at[NZ], self_s.at[g], self_r.at[g], owner)) for g in groups
    ]
    early_on = weights_on(early, 0, EARLY)

    depth = NB * ob[0].shape[1] * ROWS
    count = NZ * ROWS
    lane64 = lax.broadcasted_iota(jnp.int32, (count, 128), 1)
    b2 = []
    for g, (first, heads) in enumerate(GROUPS):
        arrive(*b1[g])
        turned = ob[g][:, :, :, heads * HD :].astype(F32).reshape(depth, 128).T
        row_top = turned[0:8] + turned[8:16] + turned[16:24]
        if g == 0:
            row_request = turned[24:25] * 8.0 + turned[25:26]
            row_q = lax.broadcasted_iota(jnp.int32, (count, depth), 0)
            my_request = (
                lax.rem(row_q // ROWS + 4, NZ) * 64 + b * ROWS + lax.rem(row_q, ROWS) + 8
            ).astype(F32)
            match = jnp.broadcast_to(row_request, (count, depth)) == my_request
        tops = jnp.full((count, 128), FLOOR, F32)
        for h in range(heads):
            level = jnp.where(match, jnp.broadcast_to(row_top[h : h + 1], (count, depth)), FLOOR)
            top = jnp.max(level, axis=1, keepdims=True)
            weight = jnp.where(match, jnp.exp(level - top), 0.0).astype(BF16)
            total = jnp.sum(weight.astype(F32), axis=1, keepdims=True)
            rows = ob[g][:, :, :, head_at(h)].astype(F32).reshape(depth, HD).astype(BF16)
            some = total > 0.0
            safe = jnp.where(some, total, 1.0)
            part = jnp.dot(weight, rows, preferred_element_type=F32) / safe
            cb[g][:, :, head_at(h)] = part.reshape(NZ, ROWS, HD).astype(BF16)
            tops = jnp.where(lane64 == h, jnp.where(some, top + jnp.log(safe), FLOOR), tops)
        cb[g][:, :, heads * HD :] = split3(tops).reshape(NZ, ROWS, 128).astype(BF16)
        b2.append(
            [
                go(
                    to_kv(
                        cb[g].at[z_at(d)], rb[g].at[z], b2_s.at[g * 8 + d], b2_r.at[g * 8 + d],
                        z_peer(d),
                    )
                )
                for d in FAR_FIRST
            ]
        )
        rb[g][z] = cb[g][z]
    late = weights_x(EARLY, chunks)

    b3 = []
    for g, (first, heads) in enumerate(GROUPS):
        arrive(*b2[g], self_copies[g])
        level = join3(rb[g][:, :, heads * HD :].astype(F32))
        share = jnp.exp(level - jnp.max(level, axis=0, keepdims=True))
        share = share / jnp.sum(share, axis=0, keepdims=True)
        for h in range(heads):
            part = share[:, :, h : h + 1] * rb[g][:, :, head_at(h)].astype(F32)
            az[g][z, :, head_at(h)] = jnp.sum(part, axis=0).astype(BF16)
        b3.append(
            [
                go(to_kv(az[g].at[z], az[g].at[z], b3_s.at[g * 8 + d], b3_r.at[g * 8 + d], z_peer(d)))
                for d in FAR_FIRST
            ]
        )
    late_on = weights_on(late, EARLY, chunks)
    large[0].wait()

    columns = chunks * 16

    def attended(g):
        arrive(*b3[g])
        return az[g][...].astype(F32).reshape(count, GROUPS[g][1] * HD).astype(BF16)

    def product(rows, e, g):
        block = wg[b_at(e)].reshape(columns, FEAT)[:, feats(g).start : feats(g).start + feats(g).size]
        return lax.dot_general(
            rows, block, (((1,), (1,)), ((), ())), preferred_element_type=F32
        )

    rows = attended(0)
    arrive(weight_own, *early_on, *late_on)
    for e in FAR_FIRST + (0,):
        acc[e, :, :columns] = product(rows, e, 0)
    rows = attended(1)
    c1 = []
    for e in FAR_FIRST + (0,):
        block = acc[e, :, :columns] + product(rows, e, 1)
        pc[e, :, :, :columns] = block.reshape(NZ, ROWS, columns).astype(BF16)
        for d in FAR_FIRST + (0,):
            band = lax.rem(t + d + 4, NT)
            if d == 0 and e == 0:
                fr[t * NB + b] = pc[e, band]
                continue
            pltpu.make_async_remote_copy(
                src_ref=pc.at[e, band], dst_ref=fr.at[t * NB + b], send_sem=c_s, recv_sem=c_r,
                device_id={"kv": b_peer(e), "tp": lax.rem(t + d, NT)}, device_id_type=MESH,
            ).start()
    for copy in sends:
        copy.wait_send()
    others = fr.at[pl.ds(0, NT * NB - 1)]
    every = to_kv(others, others, c_s, c_r, sibling)
    every.wait_recv()
    out_ref[...] = jnp.sum(fr[...].astype(F32).reshape(NT, NB * ROWS, 128), axis=0)
    every.wait_send()


def on_device(
    queries,
    new_keys,
    new_values,
    keys,
    values,
    slot_request,
    slot_valid,
    out_weight,
    out_bias,
    residual,
):
    slots = keys.shape[0]
    columns = out_weight.shape[1]
    pages = slots // PAGE
    blocks = pages // ROWS
    padded = 4
    vmem = pl.BlockSpec(memory_space=pltpu.VMEM)
    hbm = pl.BlockSpec(memory_space=pltpu.HBM)
    dma = pltpu.SemaphoreType.DMA

    def grouped(*lead, stats):
        return [
            pltpu.VMEM(lead + (heads * HD + (128 if stats else 0),), BF16) for _, heads in GROUPS
        ]

    projected = pl.pallas_call(
        kernel,
        out_shape=jax.ShapeDtypeStruct((NB * ROWS, 128), F32),
        in_specs=[hbm] * 8,
        out_specs=vmem,
        scratch_shapes=[
            pltpu.VMEM((ROWS, FEAT), BF16),
            pltpu.VMEM((ROWS, FEAT), BF16),
            pltpu.VMEM((slots,), jnp.int32),
            pltpu.VMEM((slots,), jnp.int32),
            pltpu.VMEM((slots, FEAT), BF16),
            pltpu.VMEM((slots, FEAT), BF16),
            pltpu.VMEM((NB, columns // 16, 16, FEAT), BF16),
            pltpu.VMEM((NB, pages, 128), F32),
            grouped(NZ, ROWS, stats=False),
            grouped(NB, blocks, ROWS, stats=False),
            grouped(NB, blocks, ROWS, stats=False),
            grouped(NB, padded, ROWS, stats=True),
            grouped(NZ, ROWS, stats=True),
            grouped(NZ + 1, ROWS, stats=True),
            grouped(ROWS, stats=True),
            grouped(NZ, ROWS, stats=False),
            pltpu.VMEM((NB, NZ * ROWS, 128), F32),
            pltpu.VMEM((NB, NZ, ROWS, 128), BF16),
            pltpu.VMEM((NT * NB, ROWS, 128), BF16),
            dma((9,)),
            dma((2 * NX,)), dma((2 * NX,)), dma((2 * NX,)), dma((2 * NX,)),
            dma((NB,)), dma((NB,)),
        ]
        + [dma((16,))] * 10
        + [dma((2,)), dma((2,)), dma, dma],
        compiler_params=pltpu.CompilerParams(
            collective_id=0, has_side_effects=True, vmem_limit_bytes=GRANT
        ),
        name="paged_decode",
    )(
        queries, new_keys, new_values, slot_request, slot_valid, keys, values,
        out_weight.T.reshape(columns // 16, 16, FEAT),
    )
    total = (
        residual.astype(F32) + projected[:, :columns] + out_bias.astype(F32)[None, :]
    )
    return total.astype(BF16)


def solution(mesh):
    placed = (
        P("kv", "tp"),
        P("kv", "tp"),
        P("kv", "tp"),
        P("kv", "tp"),
        P("kv", "tp"),
        P("kv"),
        P("kv"),
        P("tp", "kv"),
        P("kv"),
        P("tp", "kv"),
    )
    return jax.shard_map(
        on_device, mesh=mesh, in_specs=placed, out_specs=P("tp", "kv"), check_vma=False
    )
```

time: 58 us -> 54.6 us (0.941)
  Pallas kernels: 55.7 us -> 52.3 us
    pallas_call x1, Pallas kernels: 55.7 us -> 52.3 us  [on_device(): pl.pallas_call(kernel, out_shape=jax.ShapeDtypeStruct((NB * ROWS, 128), F...]
where the time goes in v3:
time: 54.6 us; the launch traced here: 54.4 us
  Pallas kernels  52.3 us (96%)
  other arithmetic  1.37 us (3%)
  local copies, waits for them, and re-layouts  0.66 us (1%)
    pallas_call x1, Pallas kernels, on_device(): pl.pallas_call(kernel, out_shape=jax.ShapeDtypeStruct((NB * ROWS, 128), F...  52.3 us
    convert_element_type x1, other arithmetic, on_device(): return total.astype(BF16)  1.37 us

profile of v3, /device:TPU:1, one launch (start us, length us, event | category | flops | bytes accessed | tf_op | source)
XLA Modules:
  0.0 54.4 jit_solution(12309840234618940085)
XLA Ops:
  0.0 0.0 copy-start.1
  0.0 0.7 %copy-done.1 = bf16[112]{0:T(256)(128)(2,1)S(1)} copy-done((bf16[112]{0:T(256)(128)(2,1)S(1)}, bf16[112]{0:T(256)(128)(2,1)}, u32[]{:S(2)}) %copy-start.1) | copy-done | bytes 248
  0.7 0.0 copy-start
  0.7 52.3 %paged_decode.1 = f32[64,128]{1,0:T(8,128)} custom-call(bf16[8,896]{1,0:T(8,128)(2,1)} %q_hbm.1, bf16[8,896]{1,0:T(8,128)(2,1)} %nk_hbm.1, bf16[8,896]{1,0:T(8,128)(2,1)} %nv_hbm.1, s32[384]{0:T(512)} %sr_hbm.1, s32[384]{0:T(512)} %sv_hbm.1, bf16[384,896]{1,0:T(8,128)(2,1)} %k_hbm.1, bf16[384,896]{1,0:T(8,128)(2,1)} %v_hbm.1, bf16[7,16,896]{2,1,0:T(8,128)(2,1)} %bitcast.3), custom_call_target="tpu_custom_call" | custom-call | tf_op jit(solution)/shard_map/paged_decode/pallas_call | solution.py:399
  53.0 0.0 copy-done
  53.0 1.4 %add_convert_fusion = bf16[64,112]{1,0:T(8,128)(2,1)} fusion(f32[64,128]{1,0:T(8,128)} %paged_decode.1, bf16[64,112]{1,0:T(8,128)(2,1)S(1)} %copy-done, f32[112]{0:T(128)S(1)} %convert_element_type.10), kind=kLoop, calls=%fused_computation | loop fusion | flops 28672 | bytes 57792 | tf_op jit(solution)/shard_map/convert_element_type | solution.py:441
  (1 shorter events, 0.0 us)
Async XLA Ops:
  0.0 0.7 %copy-start.1 = (bf16[112]{0:T(256)(128)(2,1)S(1)}, bf16[112]{0:T(256)(128)(2,1)}, u32[]{:S(2)}) copy-start(bf16[112]{0:T(256)(128)(2,1)} %param.18) | copy-start | bytes 676
  0.7 52.3 %copy-start = (bf16[64,112]{1,0:T(8,128)(2,1)S(1)}, bf16[64,112]{1,0:T(8,128)(2,1)}, u32[]{:S(2)}) copy-start(bf16[64,112]{1,0:T(8,128)(2,1)} %param.19) | copy-start | bytes 43012

commit v4 on v3

--- a/solution.py
+++ b/solution.py
@@ -21,6 +21,7 @@
 GROUPS = ((0, 4), (4, 3))
 
 FAR_FIRST = (4, 3, 5, 2, 6, 1, 7)
+X_FIRST = (2, 1, 3)
 
 EARLY = 3
 
@@ -50,9 +51,9 @@
 
 
 def kernel(
-    q_hbm, nk_hbm, nv_hbm, sr_hbm, sv_hbm, k_hbm, v_hbm, w_hbm, out_ref,
-    nk_ref, nv_ref, sr_ref, sv_ref, k_ref, v_ref, wg, idc, qz, qs, qr, ob, cb, rb, sb, az,
-    acc, pc, fr, local, w_s, w_r, f_s, f_r, id_s, id_r, a1_s, a1_r, a2_s, a2_r, b1_s, b1_r,
+    q_hbm, nk_hbm, nv_hbm, sr_hbm, sv_hbm, k_hbm, v_hbm, w_hbm, bias_hbm, out_ref,
+    bias_ref, nk_ref, nv_ref, sr_ref, sv_ref, k_ref, v_ref, wg, idc, qz, qs, qr, ob, cb, rb, sb, az,
+    acc, pc, fr, local, w_s, w_r, f_s, f_r, l_s, l_r, id_s, id_r, a1_s, a1_r, a2_s, a2_r, b1_s, b1_r,
     b2_s, b2_r, b3_s, b3_r, self_s, self_r, c_s, c_r,
 ):
     k = lax.axis_index("kv")
@@ -89,11 +90,12 @@
     owner = kv_of(lax.rem(z, 4), lax.rem(2 * x + z // 4 + 4, NZ), c)
 
     barrier = pltpu.get_barrier_semaphore()
-    for d in range(1, 8):
+    for d in FAR_FIRST:
         pl.semaphore_signal(barrier, inc=1, device_id={"kv": z_peer(d)}, device_id_type=MESH)
-    for d in range(1, 8):
-        pl.semaphore_signal(barrier, inc=1, device_id={"kv": b_peer(d)}, device_id_type=MESH)
-    for d in range(1, 8):
+    for d in range(1, NX):
+        pl.semaphore_signal(barrier, inc=1, device_id={"kv": x_peer(d)}, device_id_type=MESH)
+    pl.semaphore_signal(barrier, inc=1, device_id={"kv": sibling}, device_id_type=MESH)
+    for d in FAR_FIRST:
         pl.semaphore_signal(
             barrier, inc=1, device_id={"tp": lax.rem(t + d, NT)}, device_id_type=MESH
         )
@@ -108,8 +110,9 @@
         pltpu.make_async_copy(sv_hbm, sv_ref, local.at[1]),
         pltpu.make_async_copy(nk_hbm, nk_ref, local.at[2]),
         pltpu.make_async_copy(nv_hbm, nv_ref, local.at[3]),
+        pltpu.make_async_copy(bias_hbm, bias_ref, local.at[9]),
     ] + [
-        pltpu.make_async_copy(q_hbm.at[:, feats(g)], qz[g].at[z], local.at[4 + g]) for g in groups
+        pltpu.make_async_copy(q_hbm.at[:, feats(g)], qz[g].at[c, z], local.at[4 + g]) for g in groups
     ]
     large = [
         pltpu.make_async_copy(w_hbm, wg.at[b], local.at[6]),
@@ -130,13 +133,13 @@
         for copy in copies:
             copy.wait_recv()
 
-    pl.semaphore_wait(barrier, 21)
+    pl.semaphore_wait(barrier, 18)
 
     a1 = [
         [
             go(
                 to_kv(
-                    q_hbm.at[:, feats(g)], qz[g].at[z], a1_s.at[g * 8 + d], a1_r.at[g * 8 + d],
+                    q_hbm.at[:, feats(g)], qz[g].at[c, z], a1_s.at[g * 8 + d], a1_r.at[g * 8 + d],
                     z_peer(d),
                 )
             )
@@ -153,8 +156,8 @@
     small[0].wait()
     request_row = jnp.broadcast_to(sr_ref[...].reshape(1, slots).astype(F32), (pages, slots))
     page_request = jnp.max(jnp.where(on_page, request_row, -1.0), axis=1, keepdims=True)
-    idc[b] = jnp.broadcast_to(page_request, (pages, 128))
-    ids = [go(to_kv(idc.at[b], idc.at[b], id_s.at[e], id_r.at[e], b_peer(e))) for e in FAR_FIRST]
+    idc[x] = jnp.broadcast_to(page_request, (pages, 128))
+    ids = [go(to_kv(idc.at[x], idc.at[x], id_s.at[d], id_r.at[d], x_peer(d))) for d in X_FIRST]
 
     for load in large:
         load.start()
@@ -164,14 +167,14 @@
         sem = 0 if first == 0 else NX
         return [
             go(to_kv(w_hbm.at[part], wg.at[b, part], w_s.at[sem + d], w_r.at[sem + d], x_peer(d)))
-            for d in (2, 1, 3)
+            for d in X_FIRST
         ]
 
     def weights_on(copies, first, last):
         part = pl.ds(first, last - first)
         sem = 0 if first == 0 else NX
         done = []
-        for copy, d in zip(copies, (2, 1, 3)):
+        for copy, d in zip(copies, X_FIRST):
             arrive(copy)
             block = wg.at[lax.rem(x + NX - d, NX) * 2 + c, part]
             done.append(go(to_kv(block, block, f_s.at[sem + d], f_r.at[sem + d], sibling)))
@@ -190,42 +193,46 @@
         own = jnp.zeros((ROWS, 128), F32)
         for h in range(heads):
             new_key = nk_ref[:, head_at(first + h)].astype(F32)
-            product = qz[g][z, :, head_at(h)].astype(F32) * new_key
+            product = qz[g][c, z, :, head_at(h)].astype(F32) * new_key
             own = jnp.where(lane8 == h, jnp.sum(product, axis=1, keepdims=True) * SCALE, own)
         sb[g][:, : heads * HD] = nv_ref[:, feats(g)]
         sb[g][:, heads * HD :] = split3(own).astype(BF16)
         ob[g][:, blocks:] = jnp.zeros((NB, ob[g].shape[1] - blocks) + ob[g].shape[2:], BF16)
 
+    line_copies = []
+    for g in groups:
+        arrive(*a1[g])
+        line = qz[g].at[c]
+        line_copies.append(go(to_kv(line, line, l_s.at[g], l_r.at[g], sibling)))
+    arrive(*ids)
+    lane_q = lax.broadcasted_iota(jnp.int32, (NX * pages, 2 * NZ * ROWS), 1)
+    core = lane_q // (NZ * ROWS)
+    place = lax.rem(lane_q // ROWS, NZ) * 16 + core * ROWS + lax.rem(lane_q, ROWS)
+    wanted = idc[...].reshape(NX * pages, 128)
+    pick = jnp.where(wanted == (x * 128 + place).astype(F32), 1.0, 0.0).astype(BF16)
     a2 = []
     for g, (first, heads) in enumerate(GROUPS):
-        if g == 0:
-            arrive(*ids)
-            lane_q = lax.broadcasted_iota(jnp.int32, (NB * pages, NZ * ROWS), 1)
-            place = (lane_q // ROWS) * 16 + lax.rem(lane_q, ROWS)
-            lane_request = (x * 128 + c * ROWS + place).astype(F32)
-            wanted = idc[...].reshape(NB * pages, 128)[:, : NZ * ROWS]
-            pick = jnp.where(wanted == lane_request, 1.0, 0.0).astype(BF16)
-        arrive(*a1[g])
-        line = qz[g][...].astype(F32).reshape(NZ * ROWS, heads * HD).astype(BF16)
+        arrive(line_copies[g])
+        line = qz[g][...].astype(F32).reshape(2 * NZ * ROWS, heads * HD).astype(BF16)
         picked = jnp.dot(pick, line, preferred_element_type=F32)
-        qs[g][...] = picked.reshape(NB, blocks, ROWS, heads * HD).astype(BF16)
+        qs[g][...] = picked.reshape(NX, blocks, ROWS, heads * HD).astype(BF16)
         a2.append(
             [
                 go(
                     to_kv(
-                        qs[g].at[b_at(e)], qr[g].at[b], a2_s.at[g * 8 + e], a2_r.at[g * 8 + e],
-                        b_peer(e),
+                        qs[g].at[lax.rem(x + d, NX)], qr[g].at[x], a2_s.at[g * 8 + d],
+                        a2_r.at[g * 8 + d], x_peer(d),
                     )
                 )
-                for e in FAR_FIRST
+                for d in X_FIRST
             ]
         )
-        qr[g][b] = qs[g][b]
+        qr[g][x] = qs[g][x]
 
     large[1].wait()
     large[2].wait()
     lane24 = lax.broadcasted_iota(jnp.int32, (pages, 128), 1)
-    b1 = []
+    b1, both = [], []
     for g, (first, heads) in enumerate(GROUPS):
         arrive(*a2[g])
         queries = jnp.sum(qr[g][...].astype(F32), axis=0).reshape(pages, heads * HD).astype(BF16)
@@ -262,21 +269,30 @@
         mine = ob[g].at[b, pl.ds(0, blocks)]
         b1.append(
             [
-                go(to_kv(mine, mine, b1_s.at[g * 8 + e], b1_r.at[g * 8 + e], b_peer(e)))
-                for e in FAR_FIRST
+                go(to_kv(mine, mine, b1_s.at[g * 8 + d], b1_r.at[g * 8 + d], x_peer(d)))
+                for d in X_FIRST
             ]
         )
+        both.append([go(to_kv(mine, mine, b1_s.at[g * 8 + 4], b1_r.at[g * 8 + 4], sibling))])
     self_copies = [
         go(to_kv(sb[g], rb[g].at[NZ], self_s.at[g], self_r.at[g], owner)) for g in groups
     ]
     early_on = weights_on(early, 0, EARLY)
+
+    for g in groups:
+        for copy, d in zip(b1[g], X_FIRST):
+            arrive(copy)
+            block = ob[g].at[lax.rem(x + NX - d, NX) * 2 + c, pl.ds(0, blocks)]
+            sem = g * 8 + 4 + d
+            both[g].append(go(to_kv(block, block, b1_s.at[sem], b1_r.at[sem], sibling)))
+    late = weights_x(EARLY, chunks)
 
     depth = NB * ob[0].shape[1] * ROWS
     count = NZ * ROWS
     lane64 = lax.broadcasted_iota(jnp.int32, (count, 128), 1)
     b2 = []
     for g, (first, heads) in enumerate(GROUPS):
-        arrive(*b1[g])
+        arrive(*both[g])
         turned = ob[g][:, :, :, heads * HD :].astype(F32).reshape(depth, 128).T
         row_top = turned[0:8] + turned[8:16] + turned[16:24]
         if g == 0:
@@ -311,7 +327,6 @@
             ]
         )
         rb[g][z] = cb[g][z]
-    late = weights_x(EARLY, chunks)
 
     b3 = []
     for g, (first, heads) in enumerate(GROUPS):
@@ -366,7 +381,8 @@
     others = fr.at[pl.ds(0, NT * NB - 1)]
     every = to_kv(others, others, c_s, c_r, sibling)
     every.wait_recv()
-    out_ref[...] = jnp.sum(fr[...].astype(F32).reshape(NT, NB * ROWS, 128), axis=0)
+    summed = jnp.sum(fr[...].astype(F32).reshape(NT, NB * ROWS, 128), axis=0)
+    out_ref[:, :columns] = summed[:, :columns] + bias_ref[...].astype(F32).reshape(1, columns)
     every.wait_send()
 
 
@@ -399,9 +415,10 @@
     projected = pl.pallas_call(
         kernel,
         out_shape=jax.ShapeDtypeStruct((NB * ROWS, 128), F32),
-        in_specs=[hbm] * 8,
+        in_specs=[hbm] * 9,
         out_specs=vmem,
         scratch_shapes=[
+            pltpu.VMEM((columns,), BF16),
             pltpu.VMEM((ROWS, FEAT), BF16),
             pltpu.VMEM((ROWS, FEAT), BF16),
             pltpu.VMEM((slots,), jnp.int32),
@@ -409,10 +426,10 @@
             pltpu.VMEM((slots, FEAT), BF16),
             pltpu.VMEM((slots, FEAT), BF16),
             pltpu.VMEM((NB, columns // 16, 16, FEAT), BF16),
-            pltpu.VMEM((NB, pages, 128), F32),
-            grouped(NZ, ROWS, stats=False),
-            grouped(NB, blocks, ROWS, stats=False),
-            grouped(NB, blocks, ROWS, stats=False),
+            pltpu.VMEM((NX, pages, 128), F32),
+            grouped(2, NZ, ROWS, stats=False),
+            grouped(NX, blocks, ROWS, stats=False),
+            grouped(NX, blocks, ROWS, stats=False),
             grouped(NB, padded, ROWS, stats=True),
             grouped(NZ, ROWS, stats=True),
             grouped(NZ + 1, ROWS, stats=True),
@@ -421,9 +438,9 @@
             pltpu.VMEM((NB, NZ * ROWS, 128), F32),
             pltpu.VMEM((NB, NZ, ROWS, 128), BF16),
             pltpu.VMEM((NT * NB, ROWS, 128), BF16),
-            dma((9,)),
+            dma((10,)),
             dma((2 * NX,)), dma((2 * NX,)), dma((2 * NX,)), dma((2 * NX,)),
-            dma((NB,)), dma((NB,)),
+            dma((2,)), dma((2,)), dma((NX,)), dma((NX,)),
         ]
         + [dma((16,))] * 10
         + [dma((2,)), dma((2,)), dma, dma],
@@ -433,11 +450,9 @@
         name="paged_decode",
     )(
         queries, new_keys, new_values, slot_request, slot_valid, keys, values,
-        out_weight.T.reshape(columns // 16, 16, FEAT),
+        out_weight.T.reshape(columns // 16, 16, FEAT), out_bias,
     )
-    total = (
-        residual.astype(F32) + projected[:, :columns] + out_bias.astype(F32)[None, :]
-    )
+    total = residual.astype(F32) + projected[:, :columns]
     return total.astype(BF16)
 
 

time: 54.6 us -> 53.3 us (0.976)
  local copies, waits for them, and re-layouts: 0.66 us -> 0.01 us
  Pallas kernels: 52.3 us -> 51.7 us
    unnamed x4 -> x2, local copies, waits for them, and re-layouts: 0.66 us -> 0.01 us
    pallas_call x1, Pallas kernels: 52.3 us -> 51.7 us  [on_device(): pl.pallas_call(kernel, out_shape=jax.ShapeDtypeStruct((NB * ROWS, 128), F...]
where the time goes in v4:
time: 53.3 us; the launch traced here: 53.1 us
  Pallas kernels  51.7 us (97%)
  other arithmetic  1.37 us (3%)
    pallas_call x1, Pallas kernels, on_device(): pl.pallas_call(kernel, out_shape=jax.ShapeDtypeStruct((NB * ROWS, 128), F...  51.7 us
    convert_element_type x1, other arithmetic, on_device(): return total.astype(BF16)  1.37 us

profile of v4, /device:TPU:1, one launch (start us, length us, event | category | flops | bytes accessed | tf_op | source)
XLA Modules:
  0.0 53.1 jit_solution(14333069672002424307)
XLA Ops:
  0.0 0.0 copy-start
  0.0 51.7 %paged_decode.1 = f32[64,128]{1,0:T(8,128)} custom-call(bf16[8,896]{1,0:T(8,128)(2,1)} %q_hbm.1, bf16[8,896]{1,0:T(8,128)(2,1)} %nk_hbm.1, bf16[8,896]{1,0:T(8,128)(2,1)} %nv_hbm.1, s32[384]{0:T(512)} %sr_hbm.1, s32[384]{0:T(512)} %sv_hbm.1, bf16[384,896]{1,0:T(8,128)(2,1)} %k_hbm.1, bf16[384,896]{1,0:T(8,128)(2,1)} %v_hbm.1, bf16[7,16,896]{2,1,0:T(8,128)(2,1)} %bitcast.3, ...), custom_call_target="tpu_custom_call" | custom-call | tf_op jit(solution)/shard_map/paged_decode/pallas_call | solution.py:415
  51.7 0.0 copy-done
  51.7 1.4 %add_convert_fusion = bf16[64,112]{1,0:T(8,128)(2,1)} fusion(f32[64,128]{1,0:T(8,128)} %paged_decode.1, bf16[64,112]{1,0:T(8,128)(2,1)S(1)} %copy-done), kind=kLoop, calls=%fused_computation | loop fusion | flops 21504 | bytes 57344 | tf_op jit(solution)/shard_map/convert_element_type | solution.py:456
Async XLA Ops:
  0.0 51.7 %copy-start = (bf16[64,112]{1,0:T(8,128)(2,1)S(1)}, bf16[64,112]{1,0:T(8,128)(2,1)}, u32[]{:S(2)}) copy-start(bf16[64,112]{1,0:T(8,128)(2,1)} %param.19) | copy-start | bytes 43012

commit v5 on v4

--- a/solution.py
+++ b/solution.py
@@ -18,7 +18,7 @@
 MESH = pl.DeviceIdType.MESH
 F32, BF16 = jnp.float32, jnp.bfloat16
 
-GROUPS = ((0, 4), (4, 3))
+GROUPS = ((0, 3), (3, 4))
 
 FAR_FIRST = (4, 3, 5, 2, 6, 1, 7)
 X_FIRST = (2, 1, 3)

time: 53.3 us -> 52.4 us (0.983)
  Pallas kernels: 51.7 us -> 50.8 us
    pallas_call x1, Pallas kernels: 51.7 us -> 50.8 us  [on_device(): pl.pallas_call(kernel, out_shape=jax.ShapeDtypeStruct((NB * ROWS, 128), F...]
where the time goes in v5:
time: 52.4 us; the launch traced here: 52.2 us
  Pallas kernels  50.8 us (97%)
  other arithmetic  1.37 us (3%)
    pallas_call x1, Pallas kernels, on_device(): pl.pallas_call(kernel, out_shape=jax.ShapeDtypeStruct((NB * ROWS, 128), F...  50.8 us
    convert_element_type x1, other arithmetic, on_device(): return total.astype(BF16)  1.37 us

profile of v5, /device:TPU:1, one launch (start us, length us, event | category | flops | bytes accessed | tf_op | source)
XLA Modules:
  0.0 52.2 jit_solution(13751068176742560772)
XLA Ops:
  0.0 0.0 copy-start
  0.0 50.8 %paged_decode.1 = f32[64,128]{1,0:T(8,128)} custom-call(bf16[8,896]{1,0:T(8,128)(2,1)} %q_hbm.1, bf16[8,896]{1,0:T(8,128)(2,1)} %nk_hbm.1, bf16[8,896]{1,0:T(8,128)(2,1)} %nv_hbm.1, s32[384]{0:T(512)} %sr_hbm.1, s32[384]{0:T(512)} %sv_hbm.1, bf16[384,896]{1,0:T(8,128)(2,1)} %k_hbm.1, bf16[384,896]{1,0:T(8,128)(2,1)} %v_hbm.1, bf16[7,16,896]{2,1,0:T(8,128)(2,1)} %bitcast.3, ...), custom_call_target="tpu_custom_call" | custom-call | tf_op jit(solution)/shard_map/paged_decode/pallas_call | solution.py:415
  50.8 0.0 copy-done
  50.8 1.4 %add_convert_fusion = bf16[64,112]{1,0:T(8,128)(2,1)} fusion(f32[64,128]{1,0:T(8,128)} %paged_decode.1, bf16[64,112]{1,0:T(8,128)(2,1)S(1)} %copy-done), kind=kLoop, calls=%fused_computation | loop fusion | flops 21504 | bytes 57344 | tf_op jit(solution)/shard_map/convert_element_type | solution.py:456
Async XLA Ops:
  0.0 50.8 %copy-start = (bf16[64,112]{1,0:T(8,128)(2,1)S(1)}, bf16[64,112]{1,0:T(8,128)(2,1)}, u32[]{:S(2)}) copy-start(bf16[64,112]{1,0:T(8,128)(2,1)} %param.19) | copy-start | bytes 43012

commit v6 on v5

--- a/solution.py
+++ b/solution.py
@@ -18,7 +18,7 @@
 MESH = pl.DeviceIdType.MESH
 F32, BF16 = jnp.float32, jnp.bfloat16
 
-GROUPS = ((0, 3), (3, 4))
+GROUPS = ((0, 2), (2, 5))
 
 FAR_FIRST = (4, 3, 5, 2, 6, 1, 7)
 X_FIRST = (2, 1, 3)

time: 52.4 us -> 52.4 us (level)
  no operation moved by 1% of the time
where the time goes in v6:
time: 52.4 us; the launch traced here: 52.2 us
  Pallas kernels  50.8 us (97%)
  other arithmetic  1.37 us (3%)
    pallas_call x1, Pallas kernels, on_device(): pl.pallas_call(kernel, out_shape=jax.ShapeDtypeStruct((NB * ROWS, 128), F...  50.8 us
    convert_element_type x1, other arithmetic, on_device(): return total.astype(BF16)  1.37 us

profile of v6, /device:TPU:1, one launch (start us, length us, event | category | flops | bytes accessed | tf_op | source)
XLA Modules:
  0.0 52.2 jit_solution(16311000686321319224)
XLA Ops:
  0.0 0.0 copy-start
  0.0 50.8 %paged_decode.1 = f32[64,128]{1,0:T(8,128)} custom-call(bf16[8,896]{1,0:T(8,128)(2,1)} %q_hbm.1, bf16[8,896]{1,0:T(8,128)(2,1)} %nk_hbm.1, bf16[8,896]{1,0:T(8,128)(2,1)} %nv_hbm.1, s32[384]{0:T(512)} %sr_hbm.1, s32[384]{0:T(512)} %sv_hbm.1, bf16[384,896]{1,0:T(8,128)(2,1)} %k_hbm.1, bf16[384,896]{1,0:T(8,128)(2,1)} %v_hbm.1, bf16[7,16,896]{2,1,0:T(8,128)(2,1)} %bitcast.3, ...), custom_call_target="tpu_custom_call" | custom-call | tf_op jit(solution)/shard_map/paged_decode/pallas_call | solution.py:415
  50.8 0.0 copy-done
  50.8 1.4 %add_convert_fusion = bf16[64,112]{1,0:T(8,128)(2,1)} fusion(f32[64,128]{1,0:T(8,128)} %paged_decode.1, bf16[64,112]{1,0:T(8,128)(2,1)S(1)} %copy-done), kind=kLoop, calls=%fused_computation | loop fusion | flops 21504 | bytes 57344 | tf_op jit(solution)/shard_map/convert_element_type | solution.py:456
Async XLA Ops:
  0.0 50.8 %copy-start = (bf16[64,112]{1,0:T(8,128)(2,1)S(1)}, bf16[64,112]{1,0:T(8,128)(2,1)}, u32[]{:S(2)}) copy-start(bf16[64,112]{1,0:T(8,128)(2,1)} %param.19) | copy-start | bytes 43012
